TPU v7x, 32 devices: a whole 2x2x4 slice. The times are simulated.
32 devices in a mesh: section: 2 (over x), dp: 4 (over z), mp: 4 (over y, core).
Axes of the slice: x: 2, y: 2, z: 4, core: 2. Of those that a mesh axis runs over, the one named last changes fastest.
Arguments:
- w_query: bfloat16 [2, 4096, 4096], P('section', None, 'mp'), may hold values from -0.09375 to 0.09375
- w_key: bfloat16 [2, 4096, 1024], P('section', None, 'mp'), may hold values from -0.09375 to 0.09375
- w_value: bfloat16 [2, 4096, 1024], P('section', None, 'mp'), may hold values from -0.09375 to 0.09375
- w_out: bfloat16 [2, 4096, 4096], P('section', 'mp'), may hold values from -0.09375 to 0.09375
- norm_gain: bfloat16 [2, 4096], P('section', 'mp'), may hold values from 0.099609375 to 1.8984375
- saved_input: bfloat16 [2, 2, 4, 64, 4096], P('section', None, 'dp', None, 'mp'), may hold values from -6 to 6
- saved_query: bfloat16 [2, 2, 4, 64, 4096], P('section', None, 'dp', None, 'mp'), may hold values from -5 to 5
- saved_key: bfloat16 [2, 2, 4, 64, 1024], P('section', None, 'dp', None, 'mp'), may hold values from -5 to 5
- saved_value: bfloat16 [2, 2, 4, 64, 1024], P('section', None, 'dp', None, 'mp'), may hold values from -6 to 6
- grad_in: bfloat16 [2, 4, 64, 4096], P('section', 'dp', None, 'mp'), may hold values from -0.29882812 to 0.29882812
- fresh_grad: bfloat16 [1, 4, 64, 4096], P(None, 'dp', None, 'mp'), may hold values from -0.29882812 to 0.29882812
- features: bfloat16 [2, 4, 16, 7680], P(None, 'dp', None, 'section'), may hold values from -6 to 6
- image_pos: int32 [2, 4, 16], P(None, 'dp'), may hold values from 0 to 63, as said below
Outputs:
- proj_grad: bfloat16 [7680, 4096], P(('section', 'dp'), 'mp')
- pending: bfloat16 [2, 4, 64, 4096], P('section', 'dp', None, 'mp')
Inputs may be any that keep to these rules, and one draw needn't show every extreme that they name: `image_pos`: each row holds 16 consecutive ascending positions; the first row starts at 0 and the last ends at 63.
All inputs are finite; a program needn't handle non-finite values.
Results may differ from a plain program's by a relative error of at most 0.017.
Values may be sent and summed in bfloat16 or wider, within the bound.
A program may use at most 64 MiB of HBM per device.

v0:
```python
import functools

import jax
import jax.numpy as jnp
from jax import lax
from jax.experimental import pallas as pl
from jax.experimental.pallas import tpu as pltpu
from jax.sharding import PartitionSpec as P

HD = 128
LANES = 128
TICKS = 2
GAIN_ROWS = 16
MESH = pl.DeviceIdType.MESH
LAST = (((1,), (1,)), ((), ()))
FIRST = (((0,), (0,)), ((), ()))
PLAIN = (((1,), (0,)), ((), ()))


def mul(a, b, dims):
    return lax.dot_general(a, b, dims, preferred_element_type=jnp.float32)


def lane_sum(a):
    parts = [a[:, i : i + LANES] for i in range(0, a.shape[1], LANES)]
    return functools.reduce(lambda p, q: p + q, parts)


def kernel(
    n_section, n_dp, n_mp, pieces, halves,
    wq, wk, wv, wo, gain, x, q, k, v, g_in, fresh, feat, pos,
    feat_all, picks, pending,
    wq_s, wk_s, wv_s, wo_s, gain_s, x_s, q_s, k_s, v_s, g_s, feat_s, cut_s, pos_s,
    probs_s, attn_s, dq_s, dk_s, dv_s, out_s, send_s, recv_s, term_s, cross_s, cross_r,
    load_sem, wo_sem, wq_sem, wk_sem, wv_sem,
    ag_send, ag_recv, xg_send, xg_recv, rs_send, rs_recv, cr_send, cr_recv,
    held_send, held_recv, ft_send, ft_recv, px_send, px_recv, pz_send, pz_recv,
):
    section = lax.axis_index("section")
    seq = lax.axis_index("dp")
    me = lax.axis_index("mp")
    y, core = me // 2, me % 2
    partner = 2 * y + (1 - core)
    across = 2 * (1 - y) + core
    diag = 2 * (1 - y) + (1 - core)
    length = g_in.shape[2]
    width = g_in.shape[3]
    depth = width * n_mp
    kv_local = k.shape[4] // HD
    group = q.shape[4] // k.shape[4]
    scale = HD ** (-0.5)
    f32, bf16 = jnp.float32, jnp.bfloat16

    def remote(src, dst, ssem, rsem, where):
        return pltpu.make_async_remote_copy(
            src_ref=src, dst_ref=dst, send_sem=ssem, recv_sem=rsem,
            device_id=where, device_id_type=MESH,
        )

    loads = {}

    def load(name, src, dst, sem):
        loads[name] = pltpu.make_async_copy(src, dst, sem)
        loads[name].start()

    load("g", g_in.at[0, 0], g_s.at[0, me], load_sem.at[0])
    load("x0", x.at[0, 0, 0], x_s.at[0, me, pl.ds(0, length)], load_sem.at[1])
    load("gain", gain, gain_s, load_sem.at[2])
    load("x1", x.at[0, 1, 0], x_s.at[1, me, pl.ds(0, length)], load_sem.at[3])
    load("q", q.at[0, :, 0], q_s, load_sem.at[4])
    load("k", k.at[0, :, 0], k_s, load_sem.at[5])
    load("v", v.at[0, :, 0], v_s, load_sem.at[6])
    load("feat", feat.at[:, 0], feat_s, load_sem.at[7])
    load("pos", pos.at[:, 0], pos_s, load_sem.at[8])
    order = (me, partner, across, diag)
    for i, b in enumerate(order):
        columns = pl.ds(pl.multiple_of(b * width, width), width)
        load(f"wo{i}", wo.at[0, :, columns], wo_s.at[b], wo_sem.at[i])
    for i, b in enumerate((diag, across, partner, me)):
        rows = pl.ds(pl.multiple_of(b * width, width), width)
        load(f"wk{i}", wk.at[0, rows], wk_s.at[b], wk_sem.at[i])
        load(f"wv{i}", wv.at[0, rows], wv_s.at[b], wv_sem.at[i])
        load(f"wq{i}", wq.at[0, rows], wq_s.at[b], wq_sem.at[i])

    barrier = pltpu.get_barrier_semaphore()
    for b in (partner, across, diag):
        pl.semaphore_signal(barrier, inc=1, device_id={"mp": b}, device_id_type=MESH)
    for o in range(1, n_dp):
        pl.semaphore_signal(
            barrier, inc=1, device_id={"dp": (seq + o) % n_dp}, device_id_type=MESH
        )
    for o in range(1, n_section):
        pl.semaphore_signal(
            barrier, inc=1, device_id={"section": (section + o) % n_section}, device_id_type=MESH
        )
    pl.semaphore_wait(barrier, 3 + n_dp - 1 + n_section - 1)

    def gather_copy(buf, slot, rows, ssem, rsem, where):
        ref = buf.at[slot, rows]
        return remote(ref, ref, ssem, rsem, {"mp": where})

    def gather_start(buf, rows, ssem, rsem):
        gather_copy(buf, me, rows, ssem.at[1], rsem.at[1], across).start()
        gather_copy(buf, me, rows, ssem.at[0], rsem.at[0], partner).start()

    def gather_forward(buf, rows, ssem, rsem):
        gather_copy(buf, across, rows, ssem.at[1], rsem.at[1], across).wait_recv()
        gather_copy(buf, across, rows, ssem.at[2], rsem.at[2], partner).start()

    def gather_wait(buf, slot, which, rows, ssem, rsem):
        gather_copy(buf, slot, rows, ssem.at[which], rsem.at[which], partner).wait_recv()

    def gather_drain(buf, rows, ssem, rsem):
        for i in range(3):
            gather_copy(buf, me, rows, ssem.at[i], rsem.at[i], partner).wait_send()

    full = pl.ds(0, length)
    x_rows = (pl.ds(0, length + GAIN_ROWS), pl.ds(0, length))
    loads["g"].wait()
    gather_start(g_s.at[0], full, ag_send.at[0, 0], ag_recv.at[0, 0])
    loads["x0"].wait()
    loads["gain"].wait()
    x_s[0, me, pl.ds(length, GAIN_ROWS), :] = jnp.broadcast_to(
        gain_s[...], (GAIN_ROWS, width)
    )
    gather_start(x_s.at[0], x_rows[0], xg_send.at[0], xg_recv.at[0])
    loads["x1"].wait()
    gather_start(x_s.at[1], x_rows[1], xg_send.at[1], xg_recv.at[1])

    loads["feat"].wait()
    own_rows = feat_s.shape[2] // n_dp
    for j in range(n_dp):
        for t in range(TICKS):
            cut_s[j, pl.ds(t * feat_s.shape[1], feat_s.shape[1]), :] = feat_s[
                t, :, j * own_rows : (j + 1) * own_rows
            ]
    feat_own = pltpu.make_async_copy(cut_s.at[seq], feat_all.at[seq], load_sem.at[9])
    feat_own.start()

    def feat_copy(o):
        to = (seq + o) % n_dp
        return remote(
            cut_s.at[to], feat_all.at[seq], ft_send.at[o], ft_recv.at[o], {"dp": to}
        )

    for o in range(1, n_dp):
        feat_copy(o).start()

    loads["q"].wait()
    loads["k"].wait()
    loads["v"].wait()

    def stack(a, g):
        return jnp.concatenate(
            [a[:, (g * group + j) * HD : (g * group + j + 1) * HD] for j in range(group)], axis=0
        )

    rows_at = lax.rem(
        lax.broadcasted_iota(jnp.int32, (group * length, length), 0), jnp.int32(length)
    )
    cols_at = lax.broadcasted_iota(jnp.int32, (group * length, length), 1)
    causal = cols_at <= rows_at

    def softmax(t):
        for g in range(kv_local):
            kg = k_s[t, :, g * HD : (g + 1) * HD]
            scores = mul(stack(q_s[t], g), kg, LAST) * scale
            scores = jnp.where(causal, scores, -1e30)
            expo = jnp.exp(scores - jnp.max(scores, -1, keepdims=True))
            probs_s[t, g] = expo / jnp.sum(expo, -1, keepdims=True)

    for t in range(TICKS):
        softmax(t)

    def picks_second(t):
        @pl.when(section > 0)
        def _():
            remote(
                picks.at[seq, t], picks.at[seq, t], px_send.at[t, 0], px_recv.at[t],
                {"section": section},
            ).wait_recv()

        for o in range(1, n_dp):
            pick_copy(t, o).start()

    def pick_copy(t, o):
        to = (seq + o) % n_dp
        ref = picks.at[seq, t]
        return remote(ref, ref, pz_send.at[t, o], pz_recv.at[t, o], {"dp": to})

    def pick_spread(t, o):
        ref = picks.at[seq, t]
        return remote(ref, ref, px_send.at[t, o], px_recv.at[t], {"section": o})

    block = width // halves

    def rs_copy(t, i, h, where):
        lanes = pl.ds(h * block, block)
        return remote(
            send_s.at[t, i, :, lanes], recv_s.at[t, i, :, lanes],
            rs_send.at[t, i, h], rs_recv.at[t, i, h], {"mp": where},
        )

    def cross_copy(t, i, where):
        return remote(
            cross_s.at[t], cross_r.at[t, i], cr_send.at[t, i], cr_recv.at[t, i], {"mp": where}
        )

    part = length // pieces

    def held_copy(h):
        rows = pl.ds(h * part, part)
        return remote(
            out_s.at[0, rows], g_s.at[1, me, rows], held_send.at[h], held_recv.at[h],
            {"section": section - 1},
        )

    def finish_gather(t, rows_list):
        for h, rows in enumerate(rows_list):
            gather_forward(g_s.at[t], rows, ag_send.at[t, h], ag_recv.at[t, h])

    def tick(t):
        rows_list = [full] if t == 0 else [pl.ds(h * part, part) for h in range(pieces)]
        first = t == 0
        if t == 1:

            @pl.when(section == n_section - 1)
            def _():
                fresh_copy = pltpu.make_async_copy(
                    fresh.at[0, 0], g_s.at[1, me], load_sem.at[10]
                )
                fresh_copy.start()
                fresh_copy.wait()

            for h, rows in enumerate(rows_list):

                @pl.when(section < n_section - 1)
                def _():
                    held_copy(h).wait_recv()

                gather_start(g_s.at[1], rows, ag_send.at[1, h], ag_recv.at[1, h])
        if first:
            loads["wo0"].wait()
        d_attn = mul(g_s[t, me], wo_s[me], LAST)
        for h, rows in enumerate(rows_list):
            gather_wait(g_s.at[t], partner, 0, rows, ag_send.at[t, h], ag_recv.at[t, h])
        if first:
            loads["wo1"].wait()
        d_attn += mul(g_s[t, partner], wo_s[partner], LAST)
        finish_gather(t, rows_list)
        if first:
            loads["wo2"].wait()
        d_attn += mul(g_s[t, across], wo_s[across], LAST)
        for h, rows in enumerate(rows_list):
            gather_wait(g_s.at[t], diag, 2, rows, ag_send.at[t, h], ag_recv.at[t, h])
        if first:
            loads["wo3"].wait()
        d_attn += mul(g_s[t, diag], wo_s[diag], LAST)
        attn_s[...] = d_attn.astype(bf16)
        if not first:
            picks_second(0)

        for g in range(kv_local):
            lanes = slice(g * HD, (g + 1) * HD)
            kg, vg = k_s[t, :, lanes], v_s[t, :, lanes]
            qg = stack(q_s[t], g)
            ag = stack(attn_s[...], g)
            probs = probs_s[t, g]
            d_probs = mul(ag, vg, LAST)
            inner = jnp.sum(probs * d_probs, -1, keepdims=True)
            d_scores = (probs * (d_probs - inner) * scale).astype(bf16)
            d_query = mul(d_scores, kg, PLAIN).astype(bf16)
            for j in range(group):
                dq_s[:, (g * group + j) * HD : (g * group + j + 1) * HD] = d_query[
                    j * length : (j + 1) * length
                ]
            dk_s[:, lanes] = mul(d_scores, qg, FIRST).astype(bf16)
            dv_s[:, lanes] = mul(probs.astype(bf16), ag, FIRST).astype(bf16)

        def x_of(b):
            return x_s[t, b, pl.ds(0, length), :].astype(f32)

        def gain_of(b):
            return x_s[0, b, pl.ds(length, GAIN_ROWS), :].astype(f32)[0:1]

        def partial(i, b, h):
            if first and h == 0:
                loads[f"wk{i}"].wait()
                loads[f"wv{i}"].wait()
                loads[f"wq{i}"].wait()
            at = slice(h * block, (h + 1) * block)
            term = mul(dq_s[...], wq_s[b, at], LAST)
            term += mul(dk_s[...], wk_s[b, at], LAST)
            term += mul(dv_s[...], wv_s[b, at], LAST)
            term_s[i, :, at] = term
            return at, term

        for h in range(halves):
            at, term = partial(0, diag, h)
            send_s[t, 0, :, at] = term.astype(bf16)
            rs_copy(t, 0, h, partner).start()
        for h in range(halves):
            at, term = partial(1, across, h)
            rs_copy(t, 0, h, partner).wait_recv()
            send_s[t, 1, :, at] = (term + recv_s[t, 0, :, at].astype(f32)).astype(bf16)
            rs_copy(t, 1, h, across).start()
        for h in range(halves):
            at, term = partial(2, partner, h)
            send_s[t, 2, :, at] = term.astype(bf16)
            rs_copy(t, 2, h, partner).start()
        if first:
            gather_forward(x_s.at[0], x_rows[0], xg_send.at[0], xg_recv.at[0])
        for h in range(halves):
            partial(3, me, h)
        gather_wait(x_s.at[t], partner, 0, x_rows[t], xg_send.at[t], xg_recv.at[t])
        total = jnp.zeros((length, LANES), f32)
        for i, b in ((1, across), (2, partner), (3, me), (0, diag)):
            if i == 0:
                gather_wait(x_s.at[t], diag, 2, x_rows[t], xg_send.at[t], xg_recv.at[t])
            total += lane_sum(x_of(b) * gain_of(b) * term_s[i])
        padded = jnp.concatenate([total, jnp.zeros((LANES - length, LANES), f32)], axis=0)
        cross_s[t] = jnp.broadcast_to(
            jnp.sum(padded.T, axis=0, keepdims=True), cross_s.shape[1:]
        )
        for i, b in enumerate((partner, across, diag)):
            cross_copy(t, i, b).start()
        if first:
            gather_forward(x_s.at[1], x_rows[1], xg_send.at[1], xg_recv.at[1])
        squares = functools.reduce(
            lambda a, b: a + b, [lane_sum(x_of(b) * x_of(b)) for b in range(n_mp)]
        )
        squares = jnp.sum(squares, -1, keepdims=True)
        rstd = lax.rsqrt(squares / depth + 1e-05)
        for h in range(halves):
            rs_copy(t, 2, h, partner).wait_recv()
        for h in range(halves):
            rs_copy(t, 1, h, across).wait_recv()
        cross = cross_s[t]
        for i in range(3):
            cross_copy(t, i, partner).wait_recv()
            cross += cross_r[t, i]
        cross = jnp.broadcast_to(cross[0:1], (LANES, LANES)).T[:length, 0:1]
        factor = rstd * rstd * rstd * (cross / depth)
        for h in range(pieces if first else 1):
            rows = slice(h * part, (h + 1) * part) if first else slice(0, length)
            d_normed = (
                term_s[3, rows] + recv_s[t, 2, rows].astype(f32) + recv_s[t, 1, rows].astype(f32)
            )
            own = x_s[t, me, rows].astype(f32)
            d_input = rstd[rows] * (gain_of(me) * d_normed) - own * factor[rows]
            out_s[t, rows] = (g_s[t, me, rows].astype(f32) + d_input).astype(bf16)
            if first:

                @pl.when(section > 0)
                def _():
                    held_copy(h).start()

        if first:
            loads["pos"].wait()

        @pl.when(section == 0)
        def _():
            at = lax.broadcasted_iota(jnp.int32, (length, pos_s.shape[1]), 0)
            chosen = (at == pos_s[pl.ds(t, 1), :]).astype(f32).astype(bf16)
            picks[seq, t] = mul(chosen, out_s[t], FIRST).astype(bf16)
            for o in range(1, n_section):
                pick_spread(t, o).start()

    tick(0)
    tick(1)
    picks_second(1)
    pending[0, 0] = out_s[1]

    feat_own.wait()
    gather_drain(g_s.at[0], full, ag_send.at[0, 0], ag_recv.at[0, 0])
    for h in range(pieces):
        gather_drain(
            g_s.at[1], pl.ds(h * part, part), ag_send.at[1, h], ag_recv.at[1, h]
        )
    for t in range(TICKS):
        gather_drain(x_s.at[t], x_rows[t], xg_send.at[t], xg_recv.at[t])
        for i in range(3):
            for h in range(halves):
                rs_copy(t, i, h, partner).wait_send()
            cross_copy(t, i, partner).wait_send()

    @pl.when(section > 0)
    def _():
        for h in range(pieces):
            held_copy(h).wait_send()

    @pl.when(section == 0)
    def _():
        for t in range(TICKS):
            for o in range(1, n_section):
                pick_spread(t, o).wait_send()

    for o in range(1, n_dp):
        feat_copy(o).wait_send()
        source = (seq + n_dp - o) % n_dp
        remote(
            cut_s.at[seq], feat_all.at[source], ft_send.at[o], ft_recv.at[o], {"dp": source}
        ).wait_recv()
        for t in range(TICKS):
            pick_copy(t, o).wait_send()
            ref = picks.at[source, t]
            remote(ref, ref, pz_send.at[t, o], pz_recv.at[t, o], {"dp": source}).wait_recv()


def shards(
    w_query, w_key, w_value, w_out, norm_gain, saved_input, saved_query, saved_key,
    saved_value, grad_in, fresh_grad, features, image_pos, pieces=4, halves=1,
):
    n_section, n_dp, n_mp = (lax.axis_size(a) for a in ("section", "dp", "mp"))
    assert n_mp == 4
    length, width = grad_in.shape[2:]
    kw = saved_key.shape[4]
    kv_local = kw // HD
    group = width // kw
    images = features.shape[2]
    own_rows = features.shape[3] // n_dp
    f32, bf16 = jnp.float32, jnp.bfloat16
    vmem, dma = pltpu.VMEM, pltpu.SemaphoreType.DMA
    feat_all, picks, pending = pl.pallas_call(
        functools.partial(kernel, n_section, n_dp, n_mp, pieces, halves),
        out_shape=(
            jax.ShapeDtypeStruct((n_dp, TICKS * images, own_rows), bf16),
            jax.ShapeDtypeStruct((n_dp, TICKS, images, width), bf16),
            jax.ShapeDtypeStruct((1, 1, length, width), bf16),
        ),
        in_specs=[pl.BlockSpec(memory_space=pltpu.HBM)] * 13,
        out_specs=(pl.BlockSpec(memory_space=pltpu.VMEM),) * 3,
        scratch_shapes=[
            vmem((n_mp, width, width), bf16),
            vmem((n_mp, width, kw), bf16),
            vmem((n_mp, width, kw), bf16),
            vmem((n_mp, width, width), bf16),
            vmem((1, width), bf16),
            vmem((TICKS, n_mp, length + GAIN_ROWS, width), bf16),
            vmem((TICKS, length, width), bf16),
            vmem((TICKS, length, kw), bf16),
            vmem((TICKS, length, kw), bf16),
            vmem((TICKS, n_mp, length, width), bf16),
            vmem((TICKS, images, features.shape[3]), bf16),
            vmem((n_dp, TICKS * images, own_rows), bf16),
            vmem((TICKS, images), jnp.int32),
            vmem((TICKS, kv_local, group * length, length), f32),
            vmem((length, width), bf16),
            vmem((length, width), bf16),
            vmem((length, kw), bf16),
            vmem((length, kw), bf16),
            vmem((TICKS, length, width), bf16),
            vmem((TICKS, 3, length, width), bf16),
            vmem((TICKS, 3, length, width), bf16),
            vmem((n_mp, length, width), f32),
            vmem((TICKS, 8, LANES), f32),
            vmem((TICKS, 3, 8, LANES), f32),
            dma((11,)), dma((n_mp,)), dma((n_mp,)), dma((n_mp,)), dma((n_mp,)),
            dma((TICKS, pieces, 3)), dma((TICKS, pieces, 3)),
            dma((TICKS, 3)), dma((TICKS, 3)),
            dma((TICKS, 3, halves)), dma((TICKS, 3, halves)), dma((TICKS, 3)), dma((TICKS, 3)),
            dma((pieces,)), dma((pieces,)),
            dma((n_dp,)), dma((n_dp,)),
            dma((TICKS, n_section)), dma((TICKS,)),
            dma((TICKS, n_dp)), dma((TICKS, n_dp)),
        ],
        compiler_params=pltpu.CompilerParams(
            collective_id=0, has_side_effects=True, vmem_limit_bytes=48 * 2**20
        ),
    )(
        *[
            pltpu.with_memory_space_constraint(a, pltpu.HBM)
            for a in (
                w_query, w_key, w_value, w_out, norm_gain, saved_input, saved_query, saved_key,
                saved_value, grad_in, fresh_grad, features, image_pos,
            )
        ]
    )
    total = lax.dot_general(
        feat_all.reshape(-1, own_rows),
        picks.reshape(-1, width),
        FIRST,
        preferred_element_type=jnp.float32,
    )
    return total.astype(bf16), pending


def solution(mesh):
    in_specs = (
        P("section", None, "mp"),
        P("section", None, "mp"),
        P("section", None, "mp"),
        P("section", "mp", None),
        P("section", "mp"),
        P("section", None, "dp", None, "mp"),
        P("section", None, "dp", None, "mp"),
        P("section", None, "dp", None, "mp"),
        P("section", None, "dp", None, "mp"),
        P("section", "dp", None, "mp"),
        P(None, "dp", None, "mp"),
        P(None, "dp", None, "section"),
        P(None, "dp", None),
    )
    out_specs = (P(("section", "dp"), "mp"), P("section", "dp", None, "mp"))
    return jax.shard_map(shards, mesh=mesh, in_specs=in_specs, out_specs=out_specs, check_vma=False)
```

profile of v0, /device:TPU:0, one launch (start us, length us, event | category | flops | bytes accessed | tf_op | source)
XLA Modules:
  0.0 46.9 jit_solution(13723726633727619202)
XLA Ops:
  0.6 43.6 %shard_map.140 = (bf16[4,32,960]{2,1,0:T(8,128)(2,1)S(1)}, bf16[4,2,16,1024]{3,2,1,0:T(8,128)(2,1)S(1)}, bf16[1,1,64,1024]{3,2,1,0:T(8,128)(2,1)S(1)}) custom-call(bf16[1,4096,1024]{2,1,0:T(8,128)(2,1)} %wq.1, bf16[1,4096,256]{2,1,0:T(8,128)(2,1)} %wk.1, bf16[1,4096,256]{2,1,0:T(8,128)(2,1)} %wv.1, bf16[1,1024,4096]{2,1,0:T(8,128)(2,1)} %wo.1, ...), custom_call_target="tpu_custom_call" | custom-call | tf_op jit(solution)/shard_map/pallas_call | solution.py:424
  44.3 2.0 %convolution_convert_fusion = bf16[960,1024]{1,0:T(8,128)(2,1)} fusion(bf16[128,960]{1,0:T(8,128)(2,1)S(1)} %bitcast.4, bf16[128,1024]{1,0:T(8,128)(2,1)S(1)} %bitcast.5), kind=kOutput, calls=%fused_computation | convolution fusion | flops 252641280 | bytes 2473984 | tf_op jit(solution)/shard_map/dot_general | solution.py:479
  46.2 0.7 %copy.16 = bf16[1,1,64,1024]{3,2,1,0:T(8,128)(2,1)} copy(bf16[1,1,64,1024]{3,2,1,0:T(8,128)(2,1)S(1)} %get-tuple-element.11) | data formatting | bytes 262144
where the time goes:
time: 47.6 us; the launch traced here: 46.9 us
  Pallas kernels  43.6 us (92%)
  matrix products  1.97 us (4%)
  local copies, waits for them, and re-layouts  0.65 us (1%)
  between operations  0.64 us (1%)
    pallas_call x1, Pallas kernels, shards(): pl.pallas_call(functools.partial(kernel, n_section, n_dp, n_mp, pieces, h...  43.6 us
    dot_general x1, matrix products, shards(): lax.dot_general(feat_all.reshape(-1, own_rows), picks.reshape(-1, width),...  1.97 us

commit v1 on v0

v1 whole, which is shorter than its diff:
```python
import functools

import jax
import jax.numpy as jnp
from jax import lax
from jax.experimental import pallas as pl
from jax.experimental.pallas import tpu as pltpu
from jax.sharding import PartitionSpec as P

HD = 128
LANES = 128
TICKS = 2
MESH = pl.DeviceIdType.MESH
LAST = (((1,), (1,)), ((), ()))
FIRST = (((0,), (0,)), ((), ()))
PLAIN = (((1,), (0,)), ((), ()))


def mul(a, b, dims):
    return lax.dot_general(a, b, dims, preferred_element_type=jnp.float32)


def lane_sum(a):
    parts = [a[:, i : i + LANES] for i in range(0, a.shape[1], LANES)]
    return functools.reduce(lambda p, q: p + q, parts)


def kernel(
    n_section, n_dp, n_mp, chunks, direct, groups,
    wq, wk, wv, wo, gain, x, q, k, v, g_in, fresh, feat, pos,
    feat_all, picks, pending,
    wq_s, wk_s, wv_s, wo_s, gain_s, x_s, q_s, k_s, v_s, g_s, feat_s, cut_s, pos_s,
    probs_s, attn_s, dq_s, dk_s, dv_s, out_s, send_s, recv_s, term_s,
    scaled_s, upper_s, proj_s, fix_s, cross_s, cross_r, square_s, square_r, factor_s, factor_r,
    load_sem, g_sem, fresh_sem, wo_sem, wq_sem, wk_sem, wv_sem,
    ag_send, ag_recv, xg_send, xg_recv, up_send, up_recv, rs_send, rs_recv, cr_send, cr_recv,
    sq_send, sq_recv, fc_send, fc_recv,
    held_send, held_recv, far_send, ft_send, ft_recv, px_send, px_recv, pz_send, pz_recv,
):
    section = lax.axis_index("section")
    seq = lax.axis_index("dp")
    me = lax.axis_index("mp")
    y, core = me // 2, me % 2
    partner = 2 * y + (1 - core)
    across = 2 * (1 - y) + core
    diag = 2 * (1 - y) + (1 - core)
    length = g_in.shape[2]
    width = g_in.shape[3]
    depth = width * n_mp
    kw = k.shape[4]
    kv_local = kw // HD
    group = q.shape[4] // kw
    scale = HD ** (-0.5)
    f32, bf16 = jnp.float32, jnp.bfloat16
    last = n_section - 1

    def remote(src, dst, ssem, rsem, where):
        return pltpu.make_async_remote_copy(
            src_ref=src, dst_ref=dst, send_sem=ssem, recv_sem=rsem,
            device_id=where, device_id_type=MESH,
        )

    loads = {}

    def load(name, src, dst, sem):
        loads[name] = pltpu.make_async_copy(src, dst, sem)
        loads[name].start()

    cw = width // chunks
    spans = [pl.ds(c * cw, cw) for c in range(chunks)]
    for c in range(chunks):
        load(f"g{c}", g_in.at[0, 0, :, spans[c]], g_s.at[0, me, c], g_sem.at[c])
    load("x1", x.at[0, 1, 0], x_s.at[1], load_sem.at[3])
    load("gain", gain, gain_s, load_sem.at[2])
    load("x0", x.at[0, 0, 0], x_s.at[0], load_sem.at[1])
    load("q", q.at[0, :, 0], q_s, load_sem.at[4])
    load("k", k.at[0, :, 0], k_s, load_sem.at[5])
    load("v", v.at[0, :, 0], v_s, load_sem.at[6])
    load("feat", feat.at[:, 0], feat_s, load_sem.at[7])
    load("pos", pos.at[:, 0], pos_s, load_sem.at[8])

    def fresh_copy(c):
        return pltpu.make_async_copy(
            fresh.at[0, 0, :, spans[c]], g_s.at[1, me, c], fresh_sem.at[c]
        )

    @pl.when(section == last)
    def _():
        for c in range(chunks):
            fresh_copy(c).start()

    order = (me, partner, across, diag)
    for i, b in enumerate(order):
        columns = pl.ds(pl.multiple_of(b * width, width), width)
        load(f"wo{i}", wo.at[0, :, columns], wo_s.at[b], wo_sem.at[i])
    barrier = pltpu.get_barrier_semaphore()
    for b in (partner, across, diag):
        pl.semaphore_signal(barrier, inc=1, device_id={"mp": b}, device_id_type=MESH)
    for o in range(1, n_dp):
        pl.semaphore_signal(
            barrier, inc=1, device_id={"dp": (seq + o) % n_dp}, device_id_type=MESH
        )
    greets = n_mp - 1 + n_dp - 1 + n_section - 1
    for o in range(1, n_section):
        other = (section + o) % n_section
        pl.semaphore_signal(
            barrier, inc=1, device_id={"section": other}, device_id_type=MESH
        )
        pl.semaphore_signal(
            barrier, inc=1, device_id={"section": other, "mp": across}, device_id_type=MESH
        )
        greets += 1
    pl.semaphore_wait(barrier, greets)

    def block_copy(ref, ssem, rsem, where):
        return remote(ref, ref, ssem, rsem, {"mp": where})

    def chunk_copy(t, slot, c, which, where):
        return block_copy(g_s.at[t, slot, c], ag_send.at[t, c, which], ag_recv.at[t, c, which], where)

    def scaled_copy(slot, which, where):
        return block_copy(scaled_s.at[slot], xg_send.at[which], xg_recv.at[which], where)

    def upper_copy(far):
        where = {"section": section - 1}
        if far:
            where["mp"] = across
        return remote(
            x_s.at[0], upper_s.at[me], up_send.at[far], up_recv.at[far], where
        )

    def upper_near(slot, which):
        return block_copy(upper_s.at[slot], up_send.at[2 + which], up_recv.at[2 + which], partner)

    for c in range(chunks):
        loads[f"g{c}"].wait()
        chunk_copy(0, me, c, 1, across).start()
        chunk_copy(0, me, c, 0, partner).start()
    for i, b in enumerate((diag, across, partner, me)):
        rows = pl.ds(pl.multiple_of(b * width, width), width)
        load(f"wk{i}", wk.at[0, rows], wk_s.at[b], wk_sem.at[i])
        load(f"wv{i}", wv.at[0, rows], wv_s.at[b], wv_sem.at[i])
        load(f"wq{i}", wq.at[0, rows], wq_s.at[b], wq_sem.at[i])

    loads["x0"].wait()
    loads["x1"].wait()
    loads["gain"].wait()
    gains = gain_s[...].astype(f32)
    scaled_s[me] = (x_s[1].astype(f32) * gains).astype(bf16)

    def inputs_start():
        @pl.when(section > 0)
        def _():
            upper_copy(1).start()
            upper_copy(0).start()

        scaled_copy(me, 1, across).start()
        scaled_copy(me, 0, partner).start()

    def row_lanes(total):
        padded = jnp.concatenate([total, jnp.zeros((LANES - length, LANES), f32)], axis=0)
        return jnp.broadcast_to(jnp.sum(padded.T, axis=0, keepdims=True), (8, LANES))

    def as_column(lanes):
        return jnp.broadcast_to(lanes[0:1], (LANES, LANES)).T[:length, 0:1]

    def square_copy(i, where):
        return remote(
            square_s, square_r.at[i], sq_send.at[i], sq_recv.at[i], {"mp": where}
        )

    for t in range(TICKS):
        own = x_s[t].astype(f32)
        square_s[t] = row_lanes(lane_sum(own * own))
    for i, b in enumerate((partner, across, diag)):
        square_copy(i, b).start()

    own_rows = feat_s.shape[2] // n_dp
    feat_own = pltpu.make_async_copy(cut_s.at[seq], feat_all.at[seq], load_sem.at[9])

    def feat_copy(o):
        to = (seq + o) % n_dp
        return remote(
            cut_s.at[to], feat_all.at[seq], ft_send.at[o], ft_recv.at[o], {"dp": to}
        )

    @pl.when(section == last)
    def _():
        upper_s[me] = jnp.zeros((length, width), bf16)
        fix_s[...] = jnp.zeros(fix_s.shape, f32)
        factor_r[...] = jnp.zeros(factor_r.shape, f32)

    loads["q"].wait()
    loads["k"].wait()
    loads["v"].wait()

    def stack(a, g):
        return jnp.concatenate(
            [a[:, (g * group + j) * HD : (g * group + j + 1) * HD] for j in range(group)], axis=0
        )

    rows_at = lax.rem(
        lax.broadcasted_iota(jnp.int32, (group * length, length), 0), jnp.int32(length)
    )
    cols_at = lax.broadcasted_iota(jnp.int32, (group * length, length), 1)
    causal = cols_at <= rows_at

    def softmax(t):
        for g in range(kv_local):
            kg = k_s[t, :, g * HD : (g + 1) * HD]
            scores = mul(stack(q_s[t], g), kg, LAST) * scale
            scores = jnp.where(causal, scores, -1e30)
            expo = jnp.exp(scores - jnp.max(scores, -1, keepdims=True))
            probs_s[t, g] = expo / jnp.sum(expo, -1, keepdims=True)

    for t in range(TICKS):
        softmax(t)

    def picks_second(t):
        @pl.when(section > 0)
        def _():
            remote(
                picks.at[seq, t], picks.at[seq, t], px_send.at[t, 0], px_recv.at[t],
                {"section": section},
            ).wait_recv()

        for o in range(1, n_dp):
            pick_copy(t, o).start()

    def pick_copy(t, o):
        to = (seq + o) % n_dp
        ref = picks.at[seq, t]
        return remote(ref, ref, pz_send.at[t, o], pz_recv.at[t, o], {"dp": to})

    def pick_spread(t, o):
        ref = picks.at[seq, t]
        return remote(ref, ref, px_send.at[t, o], px_recv.at[t], {"section": o})

    def rs_copy(t, i, h, where):
        part = pl.ds(*groups[h])
        return remote(
            send_s.at[t, i, part], recv_s.at[t, i, part],
            rs_send.at[t, i, h], rs_recv.at[t, i, h], {"mp": where},
        )

    def cross_copy(t, i, where):
        return remote(
            cross_s.at[t], cross_r.at[t, i], cr_send.at[t, i], cr_recv.at[t, i], {"mp": where}
        )

    def cross_start(t, total):
        cross_s[t] = row_lanes(total)
        for i, b in enumerate((across, diag, partner)):
            cross_copy(t, i, b).start()

    def cross_wait(t):
        cross = cross_s[t]
        for i in range(n_mp - 1):
            cross_copy(t, i, partner).wait_recv()
            cross += cross_r[t, i]
        return cross

    def held_copy(c):
        return remote(
            out_s.at[0, c], g_s.at[1, me, c], held_send.at[c], held_recv.at[c],
            {"section": section - 1},
        )

    def held_far(c):
        return remote(
            out_s.at[0, c], g_s.at[1, me, c], far_send.at[c], ag_recv.at[1, c, 1],
            {"section": section - 1, "mp": across},
        )

    factor_copy = remote(
        factor_s, factor_r, fc_send, fc_recv, {"section": section - 1}
    )

    def wo_part(t, b, c, n=1):
        rows = [g_s[t, b, c + i] for i in range(n)]
        lhs = rows[0] if n == 1 else jnp.concatenate(rows, axis=1)
        return mul(lhs, wo_s[b, :, c * cw : (c + n) * cw], LAST)

    def arrived(t, slot, which, c):
        chunk_copy(t, slot, c, which, partner).wait_recv()

    def forward(t, c):
        arrived(t, across, 1, c)
        chunk_copy(t, across, c, 2, partner).start()

    def project():
        scaled_copy(across, 1, partner).wait_recv()
        scaled_copy(across, 2, partner).start()
        scaled_copy(partner, 0, partner).wait_recv()
        weights = ((0, wq_s), (width, wk_s), (width + kw, wv_s))
        for at, w in weights:
            total = mul(scaled_s[me], w[me], PLAIN)
            for b in (partner, across):
                total += mul(scaled_s[b], w[b], PLAIN)
            proj_s[:, at : at + w.shape[2]] = total
        scaled_copy(diag, 2, partner).wait_recv()
        for at, w in weights:
            proj_s[:, at : at + w.shape[2]] += mul(scaled_s[diag], w[diag], PLAIN)

    def correction_first():
        upper_copy(1).wait_recv()
        upper_near(across, 1).start()
        upper_copy(0).wait_recv()
        upper_near(me, 0).start()
        total = mul(upper_s[me], wo_s[me], LAST)
        fix_s[...] = total + mul(upper_s[across], wo_s[across], LAST)

    def correction_second():
        upper_near(partner, 0).wait_recv()
        total = mul(upper_s[partner], wo_s[partner], LAST)
        upper_near(diag, 1).wait_recv()
        fix_s[...] += total + mul(upper_s[diag], wo_s[diag], LAST)

    def attention(t):
        for g in range(kv_local):
            lanes = slice(g * HD, (g + 1) * HD)
            kg, vg = k_s[t, :, lanes], v_s[t, :, lanes]
            qg = stack(q_s[t], g)
            ag = stack(attn_s[...], g)
            probs = probs_s[t, g]
            d_probs = mul(ag, vg, LAST)
            inner = jnp.sum(probs * d_probs, -1, keepdims=True)
            d_scores = (probs * (d_probs - inner) * scale).astype(bf16)
            d_query = mul(d_scores, kg, PLAIN).astype(bf16)
            for j in range(group):
                dq_s[:, (g * group + j) * HD : (g * group + j + 1) * HD] = d_query[
                    j * length : (j + 1) * length
                ]
            dk_s[:, lanes] = mul(d_scores, qg, FIRST).astype(bf16)
            dv_s[:, lanes] = mul(probs.astype(bf16), ag, FIRST).astype(bf16)

    def partial(t, i, b, low, count):
        at = slice(low * cw, (low + count) * cw)
        term = mul(dq_s[...], wq_s[b, at], LAST)
        term += mul(dk_s[...], wk_s[b, at], LAST)
        term += mul(dv_s[...], wv_s[b, at], LAST)
        return [(low + j, term[:, j * cw : (j + 1) * cw]) for j in range(count)]

    def weights_wait(t, i):
        if t == 0:
            loads[f"wk{i}"].wait()
            loads[f"wv{i}"].wait()
            loads[f"wq{i}"].wait()

    def scatter(t):
        weights_wait(t, 0)
        for h in range(len(groups)):
            for c, term in partial(t, 0, diag, *groups[h]):
                send_s[t, 0, c] = term.astype(bf16)
            rs_copy(t, 0, h, partner).start()
        weights_wait(t, 1)
        for h in range(len(groups)):
            terms = partial(t, 1, across, *groups[h])
            rs_copy(t, 0, h, partner).wait_recv()
            for c, term in terms:
                send_s[t, 1, c] = (term + recv_s[t, 0, c].astype(f32)).astype(bf16)
            rs_copy(t, 1, h, across).start()
        weights_wait(t, 2)
        for c, term in partial(t, 2, partner, 0, chunks):
            send_s[t, 2, c] = term.astype(bf16)
        for h in range(len(groups)):
            rs_copy(t, 2, h, partner).start()
        weights_wait(t, 3)
        for c, term in partial(t, 3, me, 0, chunks):
            term_s[:, c * cw : (c + 1) * cw] = term

    def rstd_lanes(t):
        squares = square_s[t] + square_r[0, t] + square_r[1, t] + square_r[2, t]
        return lax.rsqrt(squares / depth + 1e-05)

    def d_normed(t, c):
        at = slice(c * cw, (c + 1) * cw)
        return term_s[:, at] + recv_s[t, 2, c].astype(f32) + recv_s[t, 1, c].astype(f32)

    def pick(t):
        rows = jnp.concatenate([out_s[t, c] for c in range(chunks)], axis=1)
        at = lax.broadcasted_iota(jnp.int32, (length, pos_s.shape[1]), 0)
        chosen = (at == pos_s[pl.ds(t, 1), :]).astype(f32).astype(bf16)
        picks[seq, t] = mul(chosen, rows, FIRST).astype(bf16)
        for o in range(1, n_section):
            pick_spread(t, o).start()

    loads["wo0"].wait()
    d_attn = wo_part(0, me, 0, chunks)
    for c in range(chunks):
        arrived(0, partner, 0, c)
    loads["wo1"].wait()
    d_attn += wo_part(0, partner, 0, chunks)
    for c in range(chunks):
        forward(0, c)
        if c == 0:
            inputs_start()
            loads["wo2"].wait()
        d_attn += wo_part(0, across, c)
        if c > 0:
            arrived(0, diag, 2, c - 1)
            if c == 1:
                loads["wo3"].wait()
            d_attn += wo_part(0, diag, c - 1)
    arrived(0, diag, 2, chunks - 1)
    d_attn += wo_part(0, diag, chunks - 1)
    attn_s[...] = d_attn.astype(bf16)
    attention(0)
    scatter(0)
    loads["feat"].wait()
    for j in range(n_dp):
        for t in range(TICKS):
            cut_s[j, pl.ds(t * feat_s.shape[1], feat_s.shape[1]), :] = feat_s[
                t, :, j * own_rows : (j + 1) * own_rows
            ]
    feat_own.start()
    for o in range(1, n_dp):
        feat_copy(o).start()

    @pl.when(section < last)
    def _():
        project()

    for i in range(n_mp - 1):
        square_copy(i, partner).wait_recv()
    rstd = as_column(rstd_lanes(0))
    total = jnp.zeros((length, LANES), f32)
    for h, (low, count) in enumerate(groups):
        rs_copy(0, 2, h, partner).wait_recv()
        rs_copy(0, 1, h, across).wait_recv()
        for c in range(low, low + count):
            at = slice(c * cw, (c + 1) * cw)
            weighted = gains[:, at] * d_normed(0, c)
            total += lane_sum(x_s[0, :, at].astype(f32) * weighted)
            passed = g_s[0, me, c].astype(f32) + rstd * weighted
            out_s[0, c] = passed.astype(bf16)
            term_s[:, at] = passed

        @pl.when(section > 0)
        def _():
            for c in range(low, low + count):
                if c in direct:
                    held_far(c).start()
            for c in range(low, low + count):
                held_copy(c).start()

    cross_start(0, total)

    @pl.when(section == last)
    def _():
        for c in range(chunks):
            fresh_copy(c).wait()
            chunk_copy(1, me, c, 1, across).start()
            chunk_copy(1, me, c, 0, partner).start()

    def factor_make():
        rstd = rstd_lanes(0)
        factor_s[...] = rstd * rstd * rstd * (cross_wait(0) / depth)

    @pl.when(section > 0)
    def _():
        factor_make()
        factor_copy.start()

    early = [c for c in range(chunks) if c not in direct]
    late = [c for c in range(chunks) if c in direct]

    def received(c):
        held_copy(c).wait_recv()
        if c not in direct:
            chunk_copy(1, me, c, 1, across).start()
        chunk_copy(1, me, c, 0, partner).start()

    @pl.when(section < last)
    def _():
        correction_first()
        for c in early:
            received(c)
        correction_second()

    loads["pos"].wait()

    @pl.when(section == 0)
    def _():
        factor_make()
        factor = as_column(factor_s[...])
        for c in range(chunks):
            at = slice(c * cw, (c + 1) * cw)
            out_s[0, c] = (term_s[:, at] - x_s[0, :, at].astype(f32) * factor).astype(bf16)
        pick(0)

    @pl.when(section == last)
    def _():
        project()

    d_attn = jnp.zeros((length, width), f32)
    for c in early:
        d_attn += wo_part(1, me, c)
    for c in early:
        arrived(1, partner, 0, c)
        d_attn += wo_part(1, partner, c)
    for c in late:
        forward(1, c)
        d_attn += wo_part(1, across, c)
    for c in late:

        @pl.when(section < last)
        def _():
            received(c)

        d_attn += wo_part(1, me, c)
    for c in early:
        forward(1, c)
        d_attn += wo_part(1, across, c)
    for c in late:
        arrived(1, diag, 2, c)
        d_attn += wo_part(1, diag, c)
    for c in late:
        arrived(1, partner, 0, c)
        d_attn += wo_part(1, partner, c)

    @pl.when(section < last)
    def _():
        factor_copy.wait_recv()

    handed = as_column(factor_r[...])
    d_attn -= handed * fix_s[...]
    for c in early:
        arrived(1, diag, 2, c)
        d_attn += wo_part(1, diag, c)
    attn_s[...] = d_attn.astype(bf16)
    picks_second(0)
    attention(1)
    total = lane_sum(dq_s[...].astype(f32) * proj_s[:, :width])
    total += lane_sum(dk_s[...].astype(f32) * proj_s[:, width : width + kw])
    total += lane_sum(dv_s[...].astype(f32) * proj_s[:, width + kw :])
    cross_start(1, total)
    scatter(1)
    rstd = rstd_lanes(1)
    factor = as_column(rstd * rstd * rstd * (cross_wait(1) / depth))
    rstd = as_column(rstd)
    for h, (low, count) in enumerate(groups):
        rs_copy(1, 2, h, partner).wait_recv()
        rs_copy(1, 1, h, across).wait_recv()
        for c in range(low, low + count):
            at = slice(c * cw, (c + 1) * cw)
            below = g_s[1, me, c].astype(f32) - handed * upper_s[me, :, at].astype(f32)
            change = rstd * (gains[:, at] * d_normed(1, c)) - x_s[1, :, at].astype(f32) * factor
            out_s[1, c] = (below + change).astype(bf16)

    @pl.when(section == 0)
    def _():
        pick(1)

    picks_second(1)
    for c in range(chunks):
        pending[0, 0, :, c * cw : (c + 1) * cw] = out_s[1, c]

    feat_own.wait()
    for c in range(chunks):
        for which in range(3):
            chunk_copy(0, me, c, which, partner).wait_send()
        for which in (0, 2):
            chunk_copy(1, me, c, which, partner).wait_send()
        if c not in direct:
            chunk_copy(1, me, c, 1, partner).wait_send()
    for i in range(3):
        scaled_copy(me, i, partner).wait_send()
        square_copy(i, partner).wait_send()
        for t in range(TICKS):
            for h in range(len(groups)):
                rs_copy(t, i, h, partner).wait_send()
            cross_copy(t, i, partner).wait_send()

    @pl.when(section == last)
    def _():
        for c in direct:
            chunk_copy(1, me, c, 1, partner).wait_send()

    @pl.when(section < last)
    def _():
        upper_near(me, 0).wait_send()
        upper_near(me, 1).wait_send()

    @pl.when(section > 0)
    def _():
        for c in range(chunks):
            held_copy(c).wait_send()
        for c in direct:
            held_far(c).wait_send()
        upper_copy(0).wait_send()
        upper_copy(1).wait_send()
        factor_copy.wait_send()

    @pl.when(section == 0)
    def _():
        for t in range(TICKS):
            for o in range(1, n_section):
                pick_spread(t, o).wait_send()

    for o in range(1, n_dp):
        feat_copy(o).wait_send()
        source = (seq + n_dp - o) % n_dp
        remote(
            cut_s.at[seq], feat_all.at[source], ft_send.at[o], ft_recv.at[o], {"dp": source}
        ).wait_recv()
        for t in range(TICKS):
            pick_copy(t, o).wait_send()
            ref = picks.at[source, t]
            remote(ref, ref, pz_send.at[t, o], pz_recv.at[t, o], {"dp": source}).wait_recv()


def shards(
    w_query, w_key, w_value, w_out, norm_gain, saved_input, saved_query, saved_key,
    saved_value, grad_in, fresh_grad, features, image_pos, chunks=4, direct=(2, 3), groups=((0, 2), (2, 2)),
):
    n_section, n_dp, n_mp = (lax.axis_size(a) for a in ("section", "dp", "mp"))
    assert n_mp == 4
    length, width = grad_in.shape[2:]
    kw = saved_key.shape[4]
    kv_local = kw // HD
    group = width // kw
    images = features.shape[2]
    own_rows = features.shape[3] // n_dp
    f32, bf16 = jnp.float32, jnp.bfloat16
    vmem, dma = pltpu.VMEM, pltpu.SemaphoreType.DMA
    feat_all, picks, pending = pl.pallas_call(
        functools.partial(kernel, n_section, n_dp, n_mp, chunks, direct, groups),
        out_shape=(
            jax.ShapeDtypeStruct((n_dp, TICKS * images, own_rows), bf16),
            jax.ShapeDtypeStruct((n_dp, TICKS, images, width), bf16),
            jax.ShapeDtypeStruct((1, 1, length, width), bf16),
        ),
        in_specs=[pl.BlockSpec(memory_space=pltpu.HBM)] * 13,
        out_specs=(pl.BlockSpec(memory_space=pltpu.VMEM),) * 3,
        scratch_shapes=[
            vmem((n_mp, width, width), bf16),
            vmem((n_mp, width, kw), bf16),
            vmem((n_mp, width, kw), bf16),
            vmem((n_mp, width, width), bf16),
            vmem((1, width), bf16),
            vmem((TICKS, length, width), bf16),
            vmem((TICKS, length, width), bf16),
            vmem((TICKS, length, kw), bf16),
            vmem((TICKS, length, kw), bf16),
            vmem((TICKS, n_mp, chunks, length, width // chunks), bf16),
            vmem((TICKS, images, features.shape[3]), bf16),
            vmem((n_dp, TICKS * images, own_rows), bf16),
            vmem((TICKS, images), jnp.int32),
            vmem((TICKS, kv_local, group * length, length), f32),
            vmem((length, width), bf16),
            vmem((length, width), bf16),
            vmem((length, kw), bf16),
            vmem((length, kw), bf16),
            vmem((TICKS, chunks, length, width // chunks), bf16),
            vmem((TICKS, 3, chunks, length, width // chunks), bf16),
            vmem((TICKS, 3, chunks, length, width // chunks), bf16),
            vmem((length, width), f32),
            vmem((n_mp, length, width), bf16),
            vmem((n_mp, length, width), bf16),
            vmem((length, width + 2 * kw), f32),
            vmem((length, width), f32),
            vmem((TICKS, 8, LANES), f32),
            vmem((TICKS, 3, 8, LANES), f32),
            vmem((TICKS, 8, LANES), f32),
            vmem((3, TICKS, 8, LANES), f32),
            vmem((8, LANES), f32),
            vmem((8, LANES), f32),
            dma((10,)), dma((chunks,)), dma((chunks,)),
            dma((n_mp,)), dma((n_mp,)), dma((n_mp,)), dma((n_mp,)),
            dma((TICKS, chunks, 3)), dma((TICKS, chunks, 3)),
            dma((3,)), dma((3,)), dma((4,)), dma((4,)),
            dma((TICKS, 3, len(groups))), dma((TICKS, 3, len(groups))),
            dma((TICKS, 3)), dma((TICKS, 3)),
            dma((3,)), dma((3,)), dma(()), dma(()),
            dma((chunks,)), dma((chunks,)), dma((chunks,)),
            dma((n_dp,)), dma((n_dp,)),
            dma((TICKS, n_section)), dma((TICKS,)),
            dma((TICKS, n_dp)), dma((TICKS, n_dp)),
        ],
        compiler_params=pltpu.CompilerParams(
            collective_id=0, has_side_effects=True, vmem_limit_bytes=48 * 2**20
        ),
    )(
        *[
            pltpu.with_memory_space_constraint(a, pltpu.HBM)
            for a in (
                w_query, w_key, w_value, w_out, norm_gain, saved_input, saved_query, saved_key,
                saved_value, grad_in, fresh_grad, features, image_pos,
            )
        ]
    )
    total = lax.dot_general(
        feat_all.reshape(-1, own_rows),
        picks.reshape(-1, width),
        FIRST,
        preferred_element_type=jnp.float32,
    )
    return total.astype(bf16), pending


def solution(mesh):
    in_specs = (
        P("section", None, "mp"),
        P("section", None, "mp"),
        P("section", None, "mp"),
        P("section", "mp", None),
        P("section", "mp"),
        P("section", None, "dp", None, "mp"),
        P("section", None, "dp", None, "mp"),
        P("section", None, "dp", None, "mp"),
        P("section", None, "dp", None, "mp"),
        P("section", "dp", None, "mp"),
        P(None, "dp", None, "mp"),
        P(None, "dp", None, "section"),
        P(None, "dp", None),
    )
    out_specs = (P(("section", "dp"), "mp"), P("section", "dp", None, "mp"))
    return jax.shard_map(shards, mesh=mesh, in_specs=in_specs, out_specs=out_specs, check_vma=False)
```

time: 47.6 us -> 44.7 us (0.939)
  Pallas kernels: 43.6 us -> 40.6 us
    pallas_call x1, Pallas kernels: 43.6 us -> 40.6 us  [shards(): pl.pallas_call(functools.partial(kernel, n_section, n_dp, n_mp, chunks, d...]
where the time goes in v1:
time: 44.7 us; the launch traced here: 43.9 us
  Pallas kernels  40.6 us (91%)
  matrix products  1.97 us (4%)
  local copies, waits for them, and re-layouts  0.65 us (1%)
  between operations  0.64 us (1%)
    pallas_call x1, Pallas kernels, shards(): pl.pallas_call(functools.partial(kernel, n_section, n_dp, n_mp, chunks, d...  40.6 us
    dot_general x1, matrix products, shards(): lax.dot_general(feat_all.reshape(-1, own_rows), picks.reshape(-1, width),...  1.97 us

profile of v1, /device:TPU:0, one launch (start us, length us, event | category | flops | bytes accessed | tf_op | source)
XLA Modules:
  0.0 43.9 jit_solution(6957967809152912732)
XLA Ops:
  0.6 40.6 %shard_map.140 = (bf16[4,32,960]{2,1,0:T(8,128)(2,1)S(1)}, bf16[4,2,16,1024]{3,2,1,0:T(8,128)(2,1)S(1)}, bf16[1,1,64,1024]{3,2,1,0:T(8,128)(2,1)S(1)}) custom-call(bf16[1,4096,1024]{2,1,0:T(8,128)(2,1)} %wq.1, bf16[1,4096,256]{2,1,0:T(8,128)(2,1)} %wk.1, bf16[1,4096,256]{2,1,0:T(8,128)(2,1)} %wv.1, bf16[1,1024,4096]{2,1,0:T(8,128)(2,1)} %wo.1, ...), custom_call_target="tpu_custom_call" | custom-call | tf_op jit(solution)/shard_map/pallas_call | solution.py:627
  41.2 2.0 %convolution_convert_fusion = bf16[960,1024]{1,0:T(8,128)(2,1)} fusion(bf16[128,960]{1,0:T(8,128)(2,1)S(1)} %bitcast.4, bf16[128,1024]{1,0:T(8,128)(2,1)S(1)} %bitcast.5), kind=kOutput, calls=%fused_computation | convolution fusion | flops 252641280 | bytes 2473984 | tf_op jit(solution)/shard_map/dot_general | solution.py:693
  43.2 0.7 %copy.16 = bf16[1,1,64,1024]{3,2,1,0:T(8,128)(2,1)} copy(bf16[1,1,64,1024]{3,2,1,0:T(8,128)(2,1)S(1)} %get-tuple-element.11) | data formatting | bytes 262144

commit v2 on v1

--- a/solution.py
+++ b/solution.py
@@ -31,10 +31,11 @@
     feat_all, picks, pending,
     wq_s, wk_s, wv_s, wo_s, gain_s, x_s, q_s, k_s, v_s, g_s, feat_s, cut_s, pos_s,
     probs_s, attn_s, dq_s, dk_s, dv_s, out_s, send_s, recv_s, term_s,
-    scaled_s, upper_s, proj_s, fix_s, cross_s, cross_r, square_s, square_r, factor_s, factor_r,
+    scaled_s, upper_s, proj_s, cross_s, cross_r, square_s, square_r, factor_s, factor_r, gain_r, rows_s, rows_r,
     load_sem, g_sem, fresh_sem, wo_sem, wq_sem, wk_sem, wv_sem,
     ag_send, ag_recv, xg_send, xg_recv, up_send, up_recv, rs_send, rs_recv, cr_send, cr_recv,
     sq_send, sq_recv, fc_send, fc_recv,
+    gn_send, gn_recv, far_rows_send, far_rows_recv, own_rows_send, own_rows_recv,
     held_send, held_recv, far_send, ft_send, ft_recv, px_send, px_recv, pz_send, pz_recv,
 ):
     section = lax.axis_index("section")
@@ -154,6 +155,7 @@
             upper_copy(1).start()
             upper_copy(0).start()
 
+        gain_copy.start()
         scaled_copy(me, 1, across).start()
         scaled_copy(me, 0, partner).start()
 
@@ -186,8 +188,7 @@
 
     @pl.when(section == last)
     def _():
-        upper_s[me] = jnp.zeros((length, width), bf16)
-        fix_s[...] = jnp.zeros(fix_s.shape, f32)
+        upper_s[...] = jnp.zeros(upper_s.shape, bf16)
         factor_r[...] = jnp.zeros(factor_r.shape, f32)
 
     loads["q"].wait()
@@ -216,25 +217,31 @@
     for t in range(TICKS):
         softmax(t)
 
-    def picks_second(t):
-        @pl.when(section > 0)
-        def _():
-            remote(
-                picks.at[seq, t], picks.at[seq, t], px_send.at[t, 0], px_recv.at[t],
-                {"section": section},
-            ).wait_recv()
-
-        for o in range(1, n_dp):
-            pick_copy(t, o).start()
-
     def pick_copy(t, o):
         to = (seq + o) % n_dp
         ref = picks.at[seq, t]
         return remote(ref, ref, pz_send.at[t, o], pz_recv.at[t, o], {"dp": to})
 
-    def pick_spread(t, o):
-        ref = picks.at[seq, t]
-        return remote(ref, ref, px_send.at[t, o], px_recv.at[t], {"section": o})
+    def pick_spread(o):
+        ref = picks.at[seq, 0]
+        return remote(ref, ref, px_send.at[o], px_recv, {"section": o})
+
+    def far_rows(o):
+        return remote(
+            rows_s.at[0], rows_r.at[0], far_rows_send.at[o], far_rows_recv,
+            {"section": o, "mp": across},
+        )
+
+    def own_rows_copy(o):
+        return remote(
+            rows_s.at[1], rows_r.at[1], own_rows_send.at[o], own_rows_recv, {"section": o}
+        )
+
+    gain_copy = remote(gain_s, gain_r, gn_send, gn_recv, {"mp": across})
+
+    def chosen(t):
+        at = lax.broadcasted_iota(jnp.int32, (length, pos_s.shape[1]), 0)
+        return (at == pos_s[pl.ds(t, 1), :]).astype(f32).astype(bf16)
 
     def rs_copy(t, i, h, where):
         part = pl.ds(*groups[h])
@@ -302,19 +309,21 @@
         for at, w in weights:
             proj_s[:, at : at + w.shape[2]] += mul(scaled_s[diag], w[diag], PLAIN)
 
-    def correction_first():
+    def uppers_forward():
         upper_copy(1).wait_recv()
         upper_near(across, 1).start()
         upper_copy(0).wait_recv()
         upper_near(me, 0).start()
-        total = mul(upper_s[me], wo_s[me], LAST)
-        fix_s[...] = total + mul(upper_s[across], wo_s[across], LAST)
-
-    def correction_second():
+
+    def uppers_wait():
         upper_near(partner, 0).wait_recv()
-        total = mul(upper_s[partner], wo_s[partner], LAST)
         upper_near(diag, 1).wait_recv()
-        fix_s[...] += total + mul(upper_s[diag], wo_s[diag], LAST)
+
+    def stacked(b, c, n):
+        lhs = jnp.concatenate([g_s[1, b, c + i] for i in range(n)], axis=1)
+        at = slice(c * cw, (c + n) * cw)
+        both = jnp.concatenate([lhs, upper_s[b, :, at]], axis=0)
+        return mul(both, wo_s[b, :, at], LAST)
 
     def attention(t):
         for g in range(kv_local):
@@ -359,7 +368,20 @@
             rs_copy(t, 0, h, partner).wait_recv()
             for c, term in terms:
                 send_s[t, 1, c] = (term + recv_s[t, 0, c].astype(f32)).astype(bf16)
-            rs_copy(t, 1, h, across).start()
+            if t == 0:
+                rs_copy(t, 1, h, across).start()
+        if t == 1:
+
+            @pl.when(section == 0)
+            def _():
+                sums = jnp.concatenate([send_s[1, 1, c] for c in range(chunks)], axis=1)
+                sums = as_column(rstd_lanes(1)) * (gain_r[...].astype(f32) * sums.astype(f32))
+                rows_s[0] = mul(chosen(1), sums.astype(bf16), FIRST).astype(bf16)
+                for o in range(n_section - 1, -1, -1):
+                    far_rows(o).start()
+
+            for h in range(len(groups)):
+                rs_copy(t, 1, h, across).start()
         weights_wait(t, 2)
         for c, term in partial(t, 2, partner, 0, chunks):
             send_s[t, 2, c] = term.astype(bf16)
@@ -377,13 +399,17 @@
         at = slice(c * cw, (c + 1) * cw)
         return term_s[:, at] + recv_s[t, 2, c].astype(f32) + recv_s[t, 1, c].astype(f32)
 
-    def pick(t):
-        rows = jnp.concatenate([out_s[t, c] for c in range(chunks)], axis=1)
-        at = lax.broadcasted_iota(jnp.int32, (length, pos_s.shape[1]), 0)
-        chosen = (at == pos_s[pl.ds(t, 1), :]).astype(f32).astype(bf16)
-        picks[seq, t] = mul(chosen, rows, FIRST).astype(bf16)
+    def pick_first():
+        rows = jnp.concatenate([out_s[0, c] for c in range(chunks)], axis=1)
+        picks[seq, 0] = mul(chosen(0), rows, FIRST).astype(bf16)
         for o in range(1, n_section):
-            pick_spread(t, o).start()
+            pick_spread(o).start()
+
+    def picks_join(own):
+        far_rows(0).wait_recv()
+        picks[seq, 1] = (own.astype(f32) + rows_r[0].astype(f32)).astype(bf16)
+        for o in range(1, n_dp):
+            pick_copy(1, o).start()
 
     loads["wo0"].wait()
     d_attn = wo_part(0, me, 0, chunks)
@@ -417,10 +443,6 @@
     for o in range(1, n_dp):
         feat_copy(o).start()
 
-    @pl.when(section < last)
-    def _():
-        project()
-
     for i in range(n_mp - 1):
         square_copy(i, partner).wait_recv()
     rstd = as_column(rstd_lanes(0))
@@ -452,6 +474,7 @@
             fresh_copy(c).wait()
             chunk_copy(1, me, c, 1, across).start()
             chunk_copy(1, me, c, 0, partner).start()
+        project()
 
     def factor_make():
         rstd = rstd_lanes(0)
@@ -473,13 +496,21 @@
 
     @pl.when(section < last)
     def _():
-        correction_first()
+        uppers_forward()
+        project()
+        uppers_wait()
         for c in early:
             received(c)
-        correction_second()
 
     loads["pos"].wait()
 
+    pair = stacked(me, early[0], len(early))
+    for c in early:
+        arrived(1, partner, 0, c)
+    pair += stacked(partner, early[0], len(early))
+    for c in late:
+        forward(1, c)
+    pair += stacked(across, late[0], len(late))
     @pl.when(section == 0)
     def _():
         factor_make()
@@ -487,50 +518,44 @@
         for c in range(chunks):
             at = slice(c * cw, (c + 1) * cw)
             out_s[0, c] = (term_s[:, at] - x_s[0, :, at].astype(f32) * factor).astype(bf16)
-        pick(0)
-
-    @pl.when(section == last)
-    def _():
-        project()
-
-    d_attn = jnp.zeros((length, width), f32)
-    for c in early:
-        d_attn += wo_part(1, me, c)
-    for c in early:
-        arrived(1, partner, 0, c)
-        d_attn += wo_part(1, partner, c)
+        pick_first()
+
     for c in late:
-        forward(1, c)
-        d_attn += wo_part(1, across, c)
+        arrived(1, diag, 2, c)
+    pair += stacked(diag, late[0], len(late))
     for c in late:
 
         @pl.when(section < last)
         def _():
             received(c)
 
-        d_attn += wo_part(1, me, c)
+    pair += stacked(me, late[0], len(late))
     for c in early:
         forward(1, c)
-        d_attn += wo_part(1, across, c)
-    for c in late:
-        arrived(1, diag, 2, c)
-        d_attn += wo_part(1, diag, c)
+    pair += stacked(across, early[0], len(early))
     for c in late:
         arrived(1, partner, 0, c)
-        d_attn += wo_part(1, partner, c)
+    pair += stacked(partner, late[0], len(late))
 
     @pl.when(section < last)
     def _():
         factor_copy.wait_recv()
 
     handed = as_column(factor_r[...])
-    d_attn -= handed * fix_s[...]
     for c in early:
         arrived(1, diag, 2, c)
-        d_attn += wo_part(1, diag, c)
+    pair += stacked(diag, early[0], len(early))
+    d_attn = pair[:length] - handed * pair[length:]
     attn_s[...] = d_attn.astype(bf16)
-    picks_second(0)
+
+    @pl.when(section > 0)
+    def _():
+        pick_spread(0).wait_recv()
+
+    for o in range(1, n_dp):
+        pick_copy(0, o).start()
     attention(1)
+    gain_copy.wait_recv()
     total = lane_sum(dq_s[...].astype(f32) * proj_s[:, :width])
     total += lane_sum(dk_s[...].astype(f32) * proj_s[:, width : width + kw])
     total += lane_sum(dv_s[...].astype(f32) * proj_s[:, width + kw :])
@@ -539,24 +564,40 @@
     rstd = rstd_lanes(1)
     factor = as_column(rstd * rstd * rstd * (cross_wait(1) / depth))
     rstd = as_column(rstd)
+    for h in range(len(groups)):
+        rs_copy(1, 2, h, partner).wait_recv()
+    for c in range(chunks):
+        at = slice(c * cw, (c + 1) * cw)
+        below = g_s[1, me, c].astype(f32) - handed * upper_s[me, :, at].astype(f32)
+        local = term_s[:, at] + recv_s[1, 2, c].astype(f32)
+        change = rstd * (gains[:, at] * local) - x_s[1, :, at].astype(f32) * factor
+        term_s[:, at] = below + change
+
+    @pl.when(section == 0)
+    def _():
+        rows_s[1] = mul(chosen(1), term_s[...].astype(bf16), FIRST).astype(bf16)
+        for o in range(1, n_section):
+            own_rows_copy(o).start()
+        picks_join(rows_s[1])
+
     for h, (low, count) in enumerate(groups):
-        rs_copy(1, 2, h, partner).wait_recv()
         rs_copy(1, 1, h, across).wait_recv()
         for c in range(low, low + count):
             at = slice(c * cw, (c + 1) * cw)
-            below = g_s[1, me, c].astype(f32) - handed * upper_s[me, :, at].astype(f32)
-            change = rstd * (gains[:, at] * d_normed(1, c)) - x_s[1, :, at].astype(f32) * factor
-            out_s[1, c] = (below + change).astype(bf16)
-
-    @pl.when(section == 0)
-    def _():
-        pick(1)
-
-    picks_second(1)
+            out_s[1, c] = (
+                term_s[:, at] + rstd * (gains[:, at] * recv_s[1, 1, c].astype(f32))
+            ).astype(bf16)
+
+    @pl.when(section > 0)
+    def _():
+        own_rows_copy(0).wait_recv()
+        picks_join(rows_r[1])
+
     for c in range(chunks):
         pending[0, 0, :, c * cw : (c + 1) * cw] = out_s[1, c]
 
     feat_own.wait()
+    gain_copy.wait_send()
     for c in range(chunks):
         for which in range(3):
             chunk_copy(0, me, c, which, partner).wait_send()
@@ -594,9 +635,11 @@
 
     @pl.when(section == 0)
     def _():
-        for t in range(TICKS):
-            for o in range(1, n_section):
-                pick_spread(t, o).wait_send()
+        far_rows(0).wait_send()
+        for o in range(1, n_section):
+            pick_spread(o).wait_send()
+            far_rows(o).wait_send()
+            own_rows_copy(o).wait_send()
 
     for o in range(1, n_dp):
         feat_copy(o).wait_send()
@@ -610,9 +653,25 @@
             remote(ref, ref, pz_send.at[t, o], pz_recv.at[t, o], {"dp": source}).wait_recv()
 
 
+def project_kernel(bands, feat, picked, pending, out, pending_out, out_s, out_sem, pending_sem):
+    handed = pltpu.make_async_copy(pending, pending_out, pending_sem)
+    handed.start()
+    band = out.shape[0] // bands
+    lhs = feat[...].T
+    copies = []
+    for i in range(bands):
+        rows = pl.ds(i * band, band)
+        out_s[rows, :] = mul(lhs[i * band : (i + 1) * band], picked[...], PLAIN).astype(out_s.dtype)
+        copies.append(pltpu.make_async_copy(out_s.at[rows], out.at[rows], out_sem.at[i]))
+        copies[-1].start()
+    for copy in copies:
+        copy.wait()
+    handed.wait()
+
+
 def shards(
     w_query, w_key, w_value, w_out, norm_gain, saved_input, saved_query, saved_key,
-    saved_value, grad_in, fresh_grad, features, image_pos, chunks=4, direct=(2, 3), groups=((0, 2), (2, 2)),
+    saved_value, grad_in, fresh_grad, features, image_pos, chunks=4, direct=(2, 3), groups=((0, 2), (2, 2)), bands=5,
 ):
     n_section, n_dp, n_mp = (lax.axis_size(a) for a in ("section", "dp", "mp"))
     assert n_mp == 4
@@ -659,13 +718,15 @@
             vmem((n_mp, length, width), bf16),
             vmem((n_mp, length, width), bf16),
             vmem((length, width + 2 * kw), f32),
-            vmem((length, width), f32),
             vmem((TICKS, 8, LANES), f32),
             vmem((TICKS, 3, 8, LANES), f32),
             vmem((TICKS, 8, LANES), f32),
             vmem((3, TICKS, 8, LANES), f32),
             vmem((8, LANES), f32),
             vmem((8, LANES), f32),
+            vmem((1, width), bf16),
+            vmem((2, images, width), bf16),
+            vmem((2, images, width), bf16),
             dma((10,)), dma((chunks,)), dma((chunks,)),
             dma((n_mp,)), dma((n_mp,)), dma((n_mp,)), dma((n_mp,)),
             dma((TICKS, chunks, 3)), dma((TICKS, chunks, 3)),
@@ -673,9 +734,10 @@
             dma((TICKS, 3, len(groups))), dma((TICKS, 3, len(groups))),
             dma((TICKS, 3)), dma((TICKS, 3)),
             dma((3,)), dma((3,)), dma(()), dma(()),
+            dma(()), dma(()), dma((n_section,)), dma(()), dma((n_section,)), dma(()),
             dma((chunks,)), dma((chunks,)), dma((chunks,)),
             dma((n_dp,)), dma((n_dp,)),
-            dma((TICKS, n_section)), dma((TICKS,)),
+            dma((n_section,)), dma(()),
             dma((TICKS, n_dp)), dma((TICKS, n_dp)),
         ],
         compiler_params=pltpu.CompilerParams(
@@ -690,13 +752,19 @@
             )
         ]
     )
-    total = lax.dot_general(
-        feat_all.reshape(-1, own_rows),
-        picks.reshape(-1, width),
-        FIRST,
-        preferred_element_type=jnp.float32,
-    )
-    return total.astype(bf16), pending
+    return pl.pallas_call(
+        functools.partial(project_kernel, bands),
+        out_shape=(
+            jax.ShapeDtypeStruct((own_rows, width), bf16),
+            jax.ShapeDtypeStruct(pending.shape, bf16),
+        ),
+        in_specs=[pl.BlockSpec(memory_space=pltpu.VMEM)] * 3,
+        out_specs=(pl.BlockSpec(memory_space=pltpu.HBM),) * 2,
+        scratch_shapes=[
+            vmem((own_rows, width), bf16), dma((bands,)), dma(()),
+        ],
+        compiler_params=pltpu.CompilerParams(vmem_limit_bytes=8 * 2**20),
+    )(feat_all.reshape(-1, own_rows), picks.reshape(-1, width), pending)
 
 
 def solution(mesh):

time: 44.7 us -> 42.2 us (0.944)
  matrix products: 1.97 us -> 0 us
  local copies, waits for them, and re-layouts: 0.65 us -> 0 us
    dot_general x1 -> x0, matrix products: 1.97 us -> none  [shards(): lax.dot_general(feat_all.reshape(-1, own_rows), picks.reshape(-1, width),...]
    pallas_call x0 -> x1, Pallas kernels: none -> 1.61 us  [shards(): pl.pallas_call(functools.partial(project_kernel, bands), out_shape=(jax.S...]
    pallas_call x1, Pallas kernels: 40.6 us -> 39.4 us  [shards(): pl.pallas_call(functools.partial(kernel, n_section, n_dp, n_mp, chunks, d...]
    unnamed x1 -> x0, local copies, waits for them, and re-layouts: 0.65 us -> none
where the time goes in v2:
time: 42.2 us; the launch traced here: 41.8 us
  Pallas kernels  41 us (97%)
  between operations  0.8 us (2%)
    pallas_call x1, Pallas kernels, shards(): pl.pallas_call(functools.partial(kernel, n_section, n_dp, n_mp, chunks, d...  39.4 us
    pallas_call x1, Pallas kernels, shards(): pl.pallas_call(functools.partial(project_kernel, bands), out_shape=(jax.S...  1.61 us

profile of v2, /device:TPU:0, one launch (start us, length us, event | category | flops | bytes accessed | tf_op | source)
XLA Modules:
  0.0 41.8 jit_solution(5375933441837113484)
XLA Ops:
  0.6 39.4 %shard_map.140 = (bf16[4,32,960]{2,1,0:T(8,128)(2,1)S(1)}, bf16[4,2,16,1024]{3,2,1,0:T(8,128)(2,1)S(1)}, bf16[1,1,64,1024]{3,2,1,0:T(8,128)(2,1)S(1)}) custom-call(bf16[1,4096,1024]{2,1,0:T(8,128)(2,1)} %wq.1, bf16[1,4096,256]{2,1,0:T(8,128)(2,1)} %wk.1, bf16[1,4096,256]{2,1,0:T(8,128)(2,1)} %wv.1, bf16[1,1024,4096]{2,1,0:T(8,128)(2,1)} %wo.1, ...), custom_call_target="tpu_custom_call" | custom-call | tf_op jit(solution)/shard_map/pallas_call | solution.py:686
  40.0 1.6 %shard_map.141 = (bf16[960,1024]{1,0:T(8,128)(2,1)}, bf16[1,1,64,1024]{3,2,1,0:T(8,128)(2,1)}) custom-call(bf16[128,960]{1,0:T(8,128)(2,1)S(1)} %bitcast.2, bf16[128,1024]{1,0:T(8,128)(2,1)S(1)} %bitcast.3, bf16[1,1,64,1024]{3,2,1,0:T(8,128)(2,1)S(1)} %get-tuple-element.7.pending), custom_call_target="tpu_custom_call" | custom-call | tf_op jit(solution)/shard_map/pallas_call | solution.py:755

commit v3 on v2

--- a/solution.py
+++ b/solution.py
@@ -29,14 +29,12 @@
     n_section, n_dp, n_mp, chunks, direct, groups,
     wq, wk, wv, wo, gain, x, q, k, v, g_in, fresh, feat, pos,
     feat_all, picks, pending,
-    wq_s, wk_s, wv_s, wo_s, gain_s, x_s, q_s, k_s, v_s, g_s, feat_s, cut_s, pos_s,
-    probs_s, attn_s, dq_s, dk_s, dv_s, out_s, send_s, recv_s, term_s,
-    scaled_s, upper_s, proj_s, cross_s, cross_r, square_s, square_r, factor_s, factor_r, gain_r, rows_s, rows_r,
-    load_sem, g_sem, fresh_sem, wo_sem, wq_sem, wk_sem, wv_sem,
-    ag_send, ag_recv, xg_send, xg_recv, up_send, up_recv, rs_send, rs_recv, cr_send, cr_recv,
-    sq_send, sq_recv, fc_send, fc_recv,
-    gn_send, gn_recv, far_rows_send, far_rows_recv, own_rows_send, own_rows_recv,
-    held_send, held_recv, far_send, ft_send, ft_recv, px_send, px_recv, pz_send, pz_recv,
+    w_s, wo_s, gain_s, x_s, q_s, k_s, v_s, g_s, feat_s, cut_s, pos_s,
+    probs_s, attn_s, grad_s, out_s, send_s, recv_s, term_s,
+    scaled_s, upper_s, proj_s, cross_s, cross_r, square_s, square_r, factor_s, factor_r,
+    gain_r, rows_s, rows_r,
+    load_sem, wo_sem, w_sem, out_sem, across_recv, near_recv, diag_recv,
+    xg_recv, up_recv, rs_recv, cr_recv, row_recv, held_recv,
 ):
     section = lax.axis_index("section")
     seq = lax.axis_index("dp")
@@ -54,6 +52,16 @@
     scale = HD ** (-0.5)
     f32, bf16 = jnp.float32, jnp.bfloat16
     last = n_section - 1
+    (
+        S_FIRST, S_NEAR, S_EARLY, S_LATE, S_SCALED, S_UPPER, S_UPPER_NEAR, S_SUMS, S_CROSS,
+        S_SQUARE, S_HELD, S_FAR, S_FEAT, S_PICK, S_ROWS, S_GAIN, S_FACTOR,
+    ) = (out_sem.at[i] for i in range(17))
+    R_SQUARE, R_FACTOR, R_GAIN, R_FAR_ROWS, R_OWN_ROWS, R_SPREAD, R_FEAT, R_PICK = (
+        row_recv.at[i] for i in range(8)
+    )
+    early = [c for c in range(chunks) if c not in direct]
+    late = [c for c in range(chunks) if c in direct]
+    first_span, later_span = pl.ds(early[0], len(early)), pl.ds(late[0], len(late))
 
     def remote(src, dst, ssem, rsem, where):
         return pltpu.make_async_remote_copy(
@@ -70,10 +78,9 @@
     cw = width // chunks
     spans = [pl.ds(c * cw, cw) for c in range(chunks)]
     for c in range(chunks):
-        load(f"g{c}", g_in.at[0, 0, :, spans[c]], g_s.at[0, me, c], g_sem.at[c])
-    load("x1", x.at[0, 1, 0], x_s.at[1], load_sem.at[3])
+        load(f"g{c}", g_in.at[0, 0, :, spans[c]], g_s.at[0, me, c], load_sem.at[0])
     load("gain", gain, gain_s, load_sem.at[2])
-    load("x0", x.at[0, 0, 0], x_s.at[0], load_sem.at[1])
+    load("x", x.at[0, :, 0], x_s, load_sem.at[1])
     load("q", q.at[0, :, 0], q_s, load_sem.at[4])
     load("k", k.at[0, :, 0], k_s, load_sem.at[5])
     load("v", v.at[0, :, 0], v_s, load_sem.at[6])
@@ -82,7 +89,7 @@
 
     def fresh_copy(c):
         return pltpu.make_async_copy(
-            fresh.at[0, 0, :, spans[c]], g_s.at[1, me, c], fresh_sem.at[c]
+            fresh.at[0, 0, :, spans[c]], g_s.at[1, me, c], load_sem.at[3]
         )
 
     @pl.when(section == last)
@@ -116,35 +123,58 @@
     def block_copy(ref, ssem, rsem, where):
         return remote(ref, ref, ssem, rsem, {"mp": where})
 
-    def chunk_copy(t, slot, c, which, where):
-        return block_copy(g_s.at[t, slot, c], ag_send.at[t, c, which], ag_recv.at[t, c, which], where)
+    def drain(ref, sem):
+        remote(ref, ref, sem, sem, {"mp": partner}).wait_send()
+
+    def landed(ref, sem):
+        remote(ref, ref, sem, sem, {"mp": partner}).wait_recv()
+
+    def near_sem(t, c):
+        return near_recv.at[0] if t == 0 else near_recv.at[2 if c in late else 1]
+
+    def diag_sem(t, c):
+        return diag_recv.at[c] if t == 0 else diag_recv.at[chunks + (1 if c in late else 0)]
+
+    def to_across(t, c):
+        ssem = S_FIRST if t == 0 else S_LATE if c in late else S_EARLY
+        return block_copy(g_s.at[t, me, c], ssem, across_recv.at[t, c], across)
+
+    def to_partner(t, c):
+        ssem = S_FIRST if t == 0 else S_NEAR
+        return block_copy(g_s.at[t, me, c], ssem, near_sem(t, c), partner)
+
+    def forward(t, c):
+        landed(g_s.at[t, across, c], across_recv.at[t, c])
+        ssem = S_FIRST if t == 0 else S_NEAR
+        block_copy(g_s.at[t, across, c], ssem, diag_sem(t, c), partner).start()
 
     def scaled_copy(slot, which, where):
-        return block_copy(scaled_s.at[slot], xg_send.at[which], xg_recv.at[which], where)
+        return block_copy(scaled_s.at[slot], S_SCALED, xg_recv.at[which], where)
 
     def upper_copy(far):
         where = {"section": section - 1}
         if far:
             where["mp"] = across
-        return remote(
-            x_s.at[0], upper_s.at[me], up_send.at[far], up_recv.at[far], where
-        )
+        return remote(x_s.at[0], upper_s.at[me], S_UPPER, up_recv.at[far], where)
 
     def upper_near(slot, which):
-        return block_copy(upper_s.at[slot], up_send.at[2 + which], up_recv.at[2 + which], partner)
-
+        return block_copy(upper_s.at[slot], S_UPPER_NEAR, up_recv.at[2 + which], partner)
+
+    def filled(ref, sem):
+        pltpu.make_async_copy(ref, ref, sem).wait()
+
+    filled(g_s.at[0, me], load_sem.at[0])
     for c in range(chunks):
-        loads[f"g{c}"].wait()
-        chunk_copy(0, me, c, 1, across).start()
-        chunk_copy(0, me, c, 0, partner).start()
+        to_across(0, c).start()
+        to_partner(0, c).start()
     for i, b in enumerate((diag, across, partner, me)):
         rows = pl.ds(pl.multiple_of(b * width, width), width)
-        load(f"wk{i}", wk.at[0, rows], wk_s.at[b], wk_sem.at[i])
-        load(f"wv{i}", wv.at[0, rows], wv_s.at[b], wv_sem.at[i])
-        load(f"wq{i}", wq.at[0, rows], wq_s.at[b], wq_sem.at[i])
-
-    loads["x0"].wait()
-    loads["x1"].wait()
+        for name, src, low, size in (
+            ("wq", wq, 0, width), ("wk", wk, width, kw), ("wv", wv, width + kw, kw)
+        ):
+            load(f"{name}{i}", src.at[0, rows], w_s.at[b, :, pl.ds(low, size)], w_sem.at[i])
+
+    loads["x"].wait()
     loads["gain"].wait()
     gains = gain_s[...].astype(f32)
     scaled_s[me] = (x_s[1].astype(f32) * gains).astype(bf16)
@@ -168,7 +198,7 @@
 
     def square_copy(i, where):
         return remote(
-            square_s, square_r.at[i], sq_send.at[i], sq_recv.at[i], {"mp": where}
+            square_s, square_r.at[i], S_SQUARE, R_SQUARE, {"mp": where}
         )
 
     for t in range(TICKS):
@@ -178,12 +208,10 @@
         square_copy(i, b).start()
 
     own_rows = feat_s.shape[2] // n_dp
-    feat_own = pltpu.make_async_copy(cut_s.at[seq], feat_all.at[seq], load_sem.at[9])
-
     def feat_copy(o):
         to = (seq + o) % n_dp
         return remote(
-            cut_s.at[to], feat_all.at[seq], ft_send.at[o], ft_recv.at[o], {"dp": to}
+            cut_s.at[to], feat_all.at[seq], S_FEAT, R_FEAT, {"dp": to}
         )
 
     @pl.when(section == last)
@@ -220,24 +248,24 @@
     def pick_copy(t, o):
         to = (seq + o) % n_dp
         ref = picks.at[seq, t]
-        return remote(ref, ref, pz_send.at[t, o], pz_recv.at[t, o], {"dp": to})
+        return remote(ref, ref, S_PICK, R_PICK, {"dp": to})
 
     def pick_spread(o):
         ref = picks.at[seq, 0]
-        return remote(ref, ref, px_send.at[o], px_recv, {"section": o})
+        return remote(ref, ref, S_ROWS, R_SPREAD, {"section": o})
 
     def far_rows(o):
         return remote(
-            rows_s.at[0], rows_r.at[0], far_rows_send.at[o], far_rows_recv,
+            rows_s.at[0], rows_r.at[0], S_ROWS, R_FAR_ROWS,
             {"section": o, "mp": across},
         )
 
     def own_rows_copy(o):
         return remote(
-            rows_s.at[1], rows_r.at[1], own_rows_send.at[o], own_rows_recv, {"section": o}
-        )
-
-    gain_copy = remote(gain_s, gain_r, gn_send, gn_recv, {"mp": across})
+            rows_s.at[1], rows_r.at[1], S_ROWS, R_OWN_ROWS, {"section": o}
+        )
+
+    gain_copy = remote(gain_s, gain_r, S_GAIN, R_GAIN, {"mp": across})
 
     def chosen(t):
         at = lax.broadcasted_iota(jnp.int32, (length, pos_s.shape[1]), 0)
@@ -245,14 +273,14 @@
 
     def rs_copy(t, i, h, where):
         part = pl.ds(*groups[h])
+        rsem = rs_recv.at[t, 2 * len(groups)] if i == 2 else rs_recv.at[t, i * len(groups) + h]
         return remote(
-            send_s.at[t, i, part], recv_s.at[t, i, part],
-            rs_send.at[t, i, h], rs_recv.at[t, i, h], {"mp": where},
+            send_s.at[t, i, part], recv_s.at[t, i, part], S_SUMS, rsem, {"mp": where}
         )
 
     def cross_copy(t, i, where):
         return remote(
-            cross_s.at[t], cross_r.at[t, i], cr_send.at[t, i], cr_recv.at[t, i], {"mp": where}
+            cross_s.at[t], cross_r.at[t, i], S_CROSS, cr_recv.at[t], {"mp": where}
         )
 
     def cross_start(t, total):
@@ -262,25 +290,25 @@
 
     def cross_wait(t):
         cross = cross_s[t]
+        landed(cross_r.at[t], cr_recv.at[t])
         for i in range(n_mp - 1):
-            cross_copy(t, i, partner).wait_recv()
             cross += cross_r[t, i]
         return cross
 
     def held_copy(c):
         return remote(
-            out_s.at[0, c], g_s.at[1, me, c], held_send.at[c], held_recv.at[c],
+            out_s.at[0, c], g_s.at[1, me, c], S_HELD, held_recv.at[c],
             {"section": section - 1},
         )
 
     def held_far(c):
         return remote(
-            out_s.at[0, c], g_s.at[1, me, c], far_send.at[c], ag_recv.at[1, c, 1],
+            out_s.at[0, c], g_s.at[1, me, c], S_FAR, across_recv.at[1, c],
             {"section": section - 1, "mp": across},
         )
 
     factor_copy = remote(
-        factor_s, factor_r, fc_send, fc_recv, {"section": section - 1}
+        factor_s, factor_r, S_FACTOR, R_FACTOR, {"section": section - 1}
     )
 
     def wo_part(t, b, c, n=1):
@@ -288,26 +316,15 @@
         lhs = rows[0] if n == 1 else jnp.concatenate(rows, axis=1)
         return mul(lhs, wo_s[b, :, c * cw : (c + n) * cw], LAST)
 
-    def arrived(t, slot, which, c):
-        chunk_copy(t, slot, c, which, partner).wait_recv()
-
-    def forward(t, c):
-        arrived(t, across, 1, c)
-        chunk_copy(t, across, c, 2, partner).start()
-
     def project():
         scaled_copy(across, 1, partner).wait_recv()
         scaled_copy(across, 2, partner).start()
         scaled_copy(partner, 0, partner).wait_recv()
-        weights = ((0, wq_s), (width, wk_s), (width + kw, wv_s))
-        for at, w in weights:
-            total = mul(scaled_s[me], w[me], PLAIN)
-            for b in (partner, across):
-                total += mul(scaled_s[b], w[b], PLAIN)
-            proj_s[:, at : at + w.shape[2]] = total
+        total = mul(scaled_s[me], w_s[me], PLAIN)
+        for b in (partner, across):
+            total += mul(scaled_s[b], w_s[b], PLAIN)
         scaled_copy(diag, 2, partner).wait_recv()
-        for at, w in weights:
-            proj_s[:, at : at + w.shape[2]] += mul(scaled_s[diag], w[diag], PLAIN)
+        proj_s[...] = total + mul(scaled_s[diag], w_s[diag], PLAIN)
 
     def uppers_forward():
         upper_copy(1).wait_recv()
@@ -337,34 +354,36 @@
             d_scores = (probs * (d_probs - inner) * scale).astype(bf16)
             d_query = mul(d_scores, kg, PLAIN).astype(bf16)
             for j in range(group):
-                dq_s[:, (g * group + j) * HD : (g * group + j + 1) * HD] = d_query[
+                grad_s[:, (g * group + j) * HD : (g * group + j + 1) * HD] = d_query[
                     j * length : (j + 1) * length
                 ]
-            dk_s[:, lanes] = mul(d_scores, qg, FIRST).astype(bf16)
-            dv_s[:, lanes] = mul(probs.astype(bf16), ag, FIRST).astype(bf16)
-
-    def partial(t, i, b, low, count):
-        at = slice(low * cw, (low + count) * cw)
-        term = mul(dq_s[...], wq_s[b, at], LAST)
-        term += mul(dk_s[...], wk_s[b, at], LAST)
-        term += mul(dv_s[...], wv_s[b, at], LAST)
+            low = width + g * HD
+            grad_s[:, low : low + HD] = mul(d_scores, qg, FIRST).astype(bf16)
+            grad_s[:, low + kw : low + kw + HD] = mul(
+                probs.astype(bf16), ag, FIRST
+            ).astype(bf16)
+
+    def partial(b, low, count, rows):
+        return mul(rows, w_s[b, low * cw : (low + count) * cw], LAST)
+
+    def pieces(term, low, count):
         return [(low + j, term[:, j * cw : (j + 1) * cw]) for j in range(count)]
 
-    def weights_wait(t, i):
+    def weights_wait(t, i, b):
         if t == 0:
-            loads[f"wk{i}"].wait()
-            loads[f"wv{i}"].wait()
-            loads[f"wq{i}"].wait()
+            filled(w_s.at[b], w_sem.at[i])
 
     def scatter(t):
-        weights_wait(t, 0)
+        weights_wait(t, 0, diag)
         for h in range(len(groups)):
-            for c, term in partial(t, 0, diag, *groups[h]):
+            for c, term in pieces(partial(diag, *groups[h], grad_s[...]), *groups[h]):
                 send_s[t, 0, c] = term.astype(bf16)
             rs_copy(t, 0, h, partner).start()
-        weights_wait(t, 1)
+        if t == 1:
+            cross_start(1, lane_sum(grad_s[...].astype(f32) * proj_s[...]))
+        weights_wait(t, 1, across)
         for h in range(len(groups)):
-            terms = partial(t, 1, across, *groups[h])
+            terms = pieces(partial(across, *groups[h], grad_s[...]), *groups[h])
             rs_copy(t, 0, h, partner).wait_recv()
             for c, term in terms:
                 send_s[t, 1, c] = (term + recv_s[t, 0, c].astype(f32)).astype(bf16)
@@ -382,14 +401,13 @@
 
             for h in range(len(groups)):
                 rs_copy(t, 1, h, across).start()
-        weights_wait(t, 2)
-        for c, term in partial(t, 2, partner, 0, chunks):
+        weights_wait(t, 2, partner)
+        for c, term in pieces(partial(partner, 0, chunks, grad_s[...]), 0, chunks):
             send_s[t, 2, c] = term.astype(bf16)
         for h in range(len(groups)):
             rs_copy(t, 2, h, partner).start()
-        weights_wait(t, 3)
-        for c, term in partial(t, 3, me, 0, chunks):
-            term_s[:, c * cw : (c + 1) * cw] = term
+        weights_wait(t, 3, me)
+        term_s[...] = partial(me, 0, chunks, grad_s[...])
 
     def rstd_lanes(t):
         squares = square_s[t] + square_r[0, t] + square_r[1, t] + square_r[2, t]
@@ -413,8 +431,7 @@
 
     loads["wo0"].wait()
     d_attn = wo_part(0, me, 0, chunks)
-    for c in range(chunks):
-        arrived(0, partner, 0, c)
+    landed(g_s.at[0, partner], near_recv.at[0])
     loads["wo1"].wait()
     d_attn += wo_part(0, partner, 0, chunks)
     for c in range(chunks):
@@ -424,11 +441,11 @@
             loads["wo2"].wait()
         d_attn += wo_part(0, across, c)
         if c > 0:
-            arrived(0, diag, 2, c - 1)
+            landed(g_s.at[0, diag, c - 1], diag_recv.at[c - 1])
             if c == 1:
                 loads["wo3"].wait()
             d_attn += wo_part(0, diag, c - 1)
-    arrived(0, diag, 2, chunks - 1)
+    landed(g_s.at[0, diag, chunks - 1], diag_recv.at[chunks - 1])
     d_attn += wo_part(0, diag, chunks - 1)
     attn_s[...] = d_attn.astype(bf16)
     attention(0)
@@ -439,16 +456,16 @@
             cut_s[j, pl.ds(t * feat_s.shape[1], feat_s.shape[1]), :] = feat_s[
                 t, :, j * own_rows : (j + 1) * own_rows
             ]
-    feat_own.start()
+    feat_all[seq] = cut_s[seq]
     for o in range(1, n_dp):
         feat_copy(o).start()
 
-    for i in range(n_mp - 1):
-        square_copy(i, partner).wait_recv()
+    landed(square_r, R_SQUARE)
     rstd = as_column(rstd_lanes(0))
     total = jnp.zeros((length, LANES), f32)
     for h, (low, count) in enumerate(groups):
-        rs_copy(0, 2, h, partner).wait_recv()
+        if h == 0:
+            landed(recv_s.at[0, 2], rs_recv.at[0, 2 * len(groups)])
         rs_copy(0, 1, h, across).wait_recv()
         for c in range(low, low + count):
             at = slice(c * cw, (c + 1) * cw)
@@ -470,10 +487,10 @@
 
     @pl.when(section == last)
     def _():
+        filled(g_s.at[1, me], load_sem.at[3])
         for c in range(chunks):
-            fresh_copy(c).wait()
-            chunk_copy(1, me, c, 1, across).start()
-            chunk_copy(1, me, c, 0, partner).start()
+            to_across(1, c).start()
+            to_partner(1, c).start()
         project()
 
     def factor_make():
@@ -485,14 +502,11 @@
         factor_make()
         factor_copy.start()
 
-    early = [c for c in range(chunks) if c not in direct]
-    late = [c for c in range(chunks) if c in direct]
-
     def received(c):
         held_copy(c).wait_recv()
         if c not in direct:
-            chunk_copy(1, me, c, 1, across).start()
-        chunk_copy(1, me, c, 0, partner).start()
+            to_across(1, c).start()
+        to_partner(1, c).start()
 
     @pl.when(section < last)
     def _():
@@ -505,12 +519,9 @@
     loads["pos"].wait()
 
     pair = stacked(me, early[0], len(early))
-    for c in early:
-        arrived(1, partner, 0, c)
+    landed(g_s.at[1, partner, first_span], near_recv.at[1])
     pair += stacked(partner, early[0], len(early))
-    for c in late:
-        forward(1, c)
-    pair += stacked(across, late[0], len(late))
+
     @pl.when(section == 0)
     def _():
         factor_make()
@@ -521,7 +532,9 @@
         pick_first()
 
     for c in late:
-        arrived(1, diag, 2, c)
+        forward(1, c)
+    pair += stacked(across, late[0], len(late))
+    landed(g_s.at[1, diag, later_span], diag_recv.at[chunks + 1])
     pair += stacked(diag, late[0], len(late))
     for c in late:
 
@@ -533,8 +546,7 @@
     for c in early:
         forward(1, c)
     pair += stacked(across, early[0], len(early))
-    for c in late:
-        arrived(1, partner, 0, c)
+    landed(g_s.at[1, partner, later_span], near_recv.at[2])
     pair += stacked(partner, late[0], len(late))
 
     @pl.when(section < last)
@@ -542,8 +554,7 @@
         factor_copy.wait_recv()
 
     handed = as_column(factor_r[...])
-    for c in early:
-        arrived(1, diag, 2, c)
+    landed(g_s.at[1, diag, first_span], diag_recv.at[chunks])
     pair += stacked(diag, early[0], len(early))
     d_attn = pair[:length] - handed * pair[length:]
     attn_s[...] = d_attn.astype(bf16)
@@ -556,16 +567,11 @@
         pick_copy(0, o).start()
     attention(1)
     gain_copy.wait_recv()
-    total = lane_sum(dq_s[...].astype(f32) * proj_s[:, :width])
-    total += lane_sum(dk_s[...].astype(f32) * proj_s[:, width : width + kw])
-    total += lane_sum(dv_s[...].astype(f32) * proj_s[:, width + kw :])
-    cross_start(1, total)
     scatter(1)
     rstd = rstd_lanes(1)
     factor = as_column(rstd * rstd * rstd * (cross_wait(1) / depth))
     rstd = as_column(rstd)
-    for h in range(len(groups)):
-        rs_copy(1, 2, h, partner).wait_recv()
+    landed(recv_s.at[1, 2], rs_recv.at[1, 2 * len(groups)])
     for c in range(chunks):
         at = slice(c * cw, (c + 1) * cw)
         below = g_s[1, me, c].astype(f32) - handed * upper_s[me, :, at].astype(f32)
@@ -596,61 +602,42 @@
     for c in range(chunks):
         pending[0, 0, :, c * cw : (c + 1) * cw] = out_s[1, c]
 
-    feat_own.wait()
-    gain_copy.wait_send()
-    for c in range(chunks):
-        for which in range(3):
-            chunk_copy(0, me, c, which, partner).wait_send()
-        for which in (0, 2):
-            chunk_copy(1, me, c, which, partner).wait_send()
-        if c not in direct:
-            chunk_copy(1, me, c, 1, partner).wait_send()
-    for i in range(3):
-        scaled_copy(me, i, partner).wait_send()
-        square_copy(i, partner).wait_send()
-        for t in range(TICKS):
-            for h in range(len(groups)):
-                rs_copy(t, i, h, partner).wait_send()
-            cross_copy(t, i, partner).wait_send()
+    drain(g_s.at[0, pl.ds(0, 3)], S_FIRST)
+    drain(g_s.at[1, pl.ds(0, 2)], S_NEAR)
+    drain(g_s.at[1, 0, first_span], S_EARLY)
+    drain(scaled_s.at[pl.ds(0, 3)], S_SCALED)
+    drain(send_s, S_SUMS)
+    drain(cross_r, S_CROSS)
+    drain(square_r, S_SQUARE)
+    drain(gain_s, S_GAIN)
 
     @pl.when(section == last)
     def _():
-        for c in direct:
-            chunk_copy(1, me, c, 1, partner).wait_send()
+        drain(g_s.at[1, 0, later_span], S_LATE)
 
     @pl.when(section < last)
     def _():
-        upper_near(me, 0).wait_send()
-        upper_near(me, 1).wait_send()
+        drain(upper_s.at[pl.ds(0, 2)], S_UPPER_NEAR)
 
     @pl.when(section > 0)
     def _():
-        for c in range(chunks):
-            held_copy(c).wait_send()
-        for c in direct:
-            held_far(c).wait_send()
-        upper_copy(0).wait_send()
-        upper_copy(1).wait_send()
-        factor_copy.wait_send()
+        drain(out_s.at[0], S_HELD)
+        drain(g_s.at[1, 0, later_span], S_FAR)
+        drain(upper_s.at[pl.ds(0, 2)], S_UPPER)
+        drain(factor_s, S_FACTOR)
 
     @pl.when(section == 0)
     def _():
-        far_rows(0).wait_send()
-        for o in range(1, n_section):
-            pick_spread(o).wait_send()
-            far_rows(o).wait_send()
-            own_rows_copy(o).wait_send()
-
-    for o in range(1, n_dp):
-        feat_copy(o).wait_send()
-        source = (seq + n_dp - o) % n_dp
-        remote(
-            cut_s.at[seq], feat_all.at[source], ft_send.at[o], ft_recv.at[o], {"dp": source}
-        ).wait_recv()
-        for t in range(TICKS):
-            pick_copy(t, o).wait_send()
-            ref = picks.at[source, t]
-            remote(ref, ref, pz_send.at[t, o], pz_recv.at[t, o], {"dp": source}).wait_recv()
+        sent = 3 * n_section - 2
+        drain(picks.at[pl.ds(0, sent // 2)], S_ROWS)
+        if sent % 2:
+            drain(picks.at[0, 0], S_ROWS)
+
+    others = pl.ds(0, n_dp - 1)
+    drain(feat_all.at[others], S_FEAT)
+    landed(feat_all.at[others], R_FEAT)
+    drain(picks.at[others], S_PICK)
+    landed(picks.at[others], R_PICK)
 
 
 def project_kernel(bands, feat, picked, pending, out, pending_out, out_s, out_sem, pending_sem):
@@ -693,9 +680,7 @@
         in_specs=[pl.BlockSpec(memory_space=pltpu.HBM)] * 13,
         out_specs=(pl.BlockSpec(memory_space=pltpu.VMEM),) * 3,
         scratch_shapes=[
-            vmem((n_mp, width, width), bf16),
-            vmem((n_mp, width, kw), bf16),
-            vmem((n_mp, width, kw), bf16),
+            vmem((n_mp, width, width + 2 * kw), bf16),
             vmem((n_mp, width, width), bf16),
             vmem((1, width), bf16),
             vmem((TICKS, length, width), bf16),
@@ -708,9 +693,7 @@
             vmem((TICKS, images), jnp.int32),
             vmem((TICKS, kv_local, group * length, length), f32),
             vmem((length, width), bf16),
-            vmem((length, width), bf16),
-            vmem((length, kw), bf16),
-            vmem((length, kw), bf16),
+            vmem((length, width + 2 * kw), bf16),
             vmem((TICKS, chunks, length, width // chunks), bf16),
             vmem((TICKS, 3, chunks, length, width // chunks), bf16),
             vmem((TICKS, 3, chunks, length, width // chunks), bf16),
@@ -727,18 +710,10 @@
             vmem((1, width), bf16),
             vmem((2, images, width), bf16),
             vmem((2, images, width), bf16),
-            dma((10,)), dma((chunks,)), dma((chunks,)),
-            dma((n_mp,)), dma((n_mp,)), dma((n_mp,)), dma((n_mp,)),
-            dma((TICKS, chunks, 3)), dma((TICKS, chunks, 3)),
-            dma((3,)), dma((3,)), dma((4,)), dma((4,)),
-            dma((TICKS, 3, len(groups))), dma((TICKS, 3, len(groups))),
-            dma((TICKS, 3)), dma((TICKS, 3)),
-            dma((3,)), dma((3,)), dma(()), dma(()),
-            dma(()), dma(()), dma((n_section,)), dma(()), dma((n_section,)), dma(()),
-            dma((chunks,)), dma((chunks,)), dma((chunks,)),
-            dma((n_dp,)), dma((n_dp,)),
-            dma((n_section,)), dma(()),
-            dma((TICKS, n_dp)), dma((TICKS, n_dp)),
+            dma((9,)), dma((n_mp,)), dma((n_mp,)), dma((17,)),
+            dma((TICKS, chunks)), dma((3,)), dma((chunks + 2,)),
+            dma((3,)), dma((4,)), dma((TICKS, 2 * len(groups) + 1)), dma((TICKS,)),
+            dma((8,)), dma((chunks,)),
         ],
         compiler_params=pltpu.CompilerParams(
             collective_id=0, has_side_effects=True, vmem_limit_bytes=48 * 2**20

time: 42.2 us -> 41.4 us (0.981)
  no operation moved by 1% of the time
where the time goes in v3:
time: 41.4 us; the launch traced here: 41.2 us
  Pallas kernels  40.6 us (98%)
  between operations  0.64 us (2%)
    pallas_call x1, Pallas kernels, shards(): pl.pallas_call(functools.partial(kernel, n_section, n_dp, n_mp, chunks, d...  39 us
    pallas_call x1, Pallas kernels, shards(): pl.pallas_call(functools.partial(project_kernel, bands), out_shape=(jax.S...  1.61 us

profile of v3, /device:TPU:0, one launch (start us, length us, event | category | flops | bytes accessed | tf_op | source)
XLA Modules:
  0.0 41.2 jit_solution(4320247181805289593)
XLA Ops:
  0.6 39.0 %shard_map.140 = (bf16[4,32,960]{2,1,0:T(8,128)(2,1)S(1)}, bf16[4,2,16,1024]{3,2,1,0:T(8,128)(2,1)S(1)}, bf16[1,1,64,1024]{3,2,1,0:T(8,128)(2,1)S(1)}) custom-call(bf16[1,4096,1024]{2,1,0:T(8,128)(2,1)} %wq.1, bf16[1,4096,256]{2,1,0:T(8,128)(2,1)} %wk.1, bf16[1,4096,256]{2,1,0:T(8,128)(2,1)} %wv.1, bf16[1,1024,4096]{2,1,0:T(8,128)(2,1)} %wo.1, ...), custom_call_target="tpu_custom_call" | custom-call | tf_op jit(solution)/shard_map/pallas_call | solution.py:673
  39.6 1.6 %shard_map.141 = (bf16[960,1024]{1,0:T(8,128)(2,1)}, bf16[1,1,64,1024]{3,2,1,0:T(8,128)(2,1)}) custom-call(bf16[128,960]{1,0:T(8,128)(2,1)S(1)} %bitcast.2, bf16[128,1024]{1,0:T(8,128)(2,1)S(1)} %bitcast.3, bf16[1,1,64,1024]{3,2,1,0:T(8,128)(2,1)S(1)} %get-tuple-element.7.pending), custom_call_target="tpu_custom_call" | custom-call | tf_op jit(solution)/shard_map/pallas_call | solution.py:730

commit v4 on v3

--- a/solution.py
+++ b/solution.py
@@ -32,9 +32,9 @@
     w_s, wo_s, gain_s, x_s, q_s, k_s, v_s, g_s, feat_s, cut_s, pos_s,
     probs_s, attn_s, grad_s, out_s, send_s, recv_s, term_s,
     scaled_s, upper_s, proj_s, cross_s, cross_r, square_s, square_r, factor_s, factor_r,
-    gain_r, rows_s, rows_r,
+    gain_r, rows_s, rows_r, base_s, sel_s, sel_r, rstd_s, bases_s,
     load_sem, wo_sem, w_sem, out_sem, across_recv, near_recv, diag_recv,
-    xg_recv, up_recv, rs_recv, cr_recv, row_recv, held_recv,
+    xg_recv, up_recv, rs_recv, cr_recv, row_recv, held_recv, sel_recv, far_recv, own_recv,
 ):
     section = lax.axis_index("section")
     seq = lax.axis_index("dp")
@@ -55,10 +55,9 @@
     (
         S_FIRST, S_NEAR, S_EARLY, S_LATE, S_SCALED, S_UPPER, S_UPPER_NEAR, S_SUMS, S_CROSS,
         S_SQUARE, S_HELD, S_FAR, S_FEAT, S_PICK, S_ROWS, S_GAIN, S_FACTOR,
-    ) = (out_sem.at[i] for i in range(17))
-    R_SQUARE, R_FACTOR, R_GAIN, R_FAR_ROWS, R_OWN_ROWS, R_SPREAD, R_FEAT, R_PICK = (
-        row_recv.at[i] for i in range(8)
-    )
+        S_CHOSEN,
+    ) = (out_sem.at[i] for i in range(18))
+    R_SQUARE, R_FACTOR, R_GAIN, R_SPREAD, R_FEAT, R_PICK = (row_recv.at[i] for i in range(6))
     early = [c for c in range(chunks) if c not in direct]
     late = [c for c in range(chunks) if c in direct]
     first_span, later_span = pl.ds(early[0], len(early)), pl.ds(late[0], len(late))
@@ -245,35 +244,38 @@
     for t in range(TICKS):
         softmax(t)
 
-    def pick_copy(t, o):
-        to = (seq + o) % n_dp
-        ref = picks.at[seq, t]
-        return remote(ref, ref, S_PICK, R_PICK, {"dp": to})
+    def pick_copy(ref, o):
+        return remote(ref, ref, S_PICK, R_PICK, {"dp": (seq + o) % n_dp})
 
     def pick_spread(o):
         ref = picks.at[seq, 0]
         return remote(ref, ref, S_ROWS, R_SPREAD, {"section": o})
 
-    def far_rows(o):
+    def far_rows(h, o):
         return remote(
-            rows_s.at[0], rows_r.at[0], S_ROWS, R_FAR_ROWS,
+            rows_s.at[0, h], rows_r.at[0, h], S_ROWS, far_recv.at[h],
             {"section": o, "mp": across},
         )
 
-    def own_rows_copy(o):
+    def own_rows_copy(h, o):
         return remote(
-            rows_s.at[1], rows_r.at[1], S_ROWS, R_OWN_ROWS, {"section": o}
+            rows_s.at[1, h], rows_r.at[1, h], S_ROWS, own_recv.at[h], {"section": o}
+        )
+
+    def sel_copy(i, h):
+        return remote(
+            sel_s.at[i, h], sel_r.at[i, h], S_CHOSEN, sel_recv.at[i, h], {"mp": partner}
         )
 
     gain_copy = remote(gain_s, gain_r, S_GAIN, R_GAIN, {"mp": across})
 
     def chosen(t):
         at = lax.broadcasted_iota(jnp.int32, (length, pos_s.shape[1]), 0)
-        return (at == pos_s[pl.ds(t, 1), :]).astype(f32).astype(bf16)
+        return (at == pos_s[pl.ds(t, 1), :]).astype(f32)
 
     def rs_copy(t, i, h, where):
-        part = pl.ds(*groups[h])
-        rsem = rs_recv.at[t, 2 * len(groups)] if i == 2 else rs_recv.at[t, i * len(groups) + h]
+        part = pl.ds(h, 1) if i == 1 else pl.ds(*groups[h])
+        rsem = rs_recv.at[t, (h, len(groups) + h, len(groups) + chunks)[i]]
         return remote(
             send_s.at[t, i, part], recv_s.at[t, i, part], S_SUMS, rsem, {"mp": where}
         )
@@ -354,12 +356,12 @@
             d_scores = (probs * (d_probs - inner) * scale).astype(bf16)
             d_query = mul(d_scores, kg, PLAIN).astype(bf16)
             for j in range(group):
-                grad_s[:, (g * group + j) * HD : (g * group + j + 1) * HD] = d_query[
+                grad_s[:length, (g * group + j) * HD : (g * group + j + 1) * HD] = d_query[
                     j * length : (j + 1) * length
                 ]
             low = width + g * HD
-            grad_s[:, low : low + HD] = mul(d_scores, qg, FIRST).astype(bf16)
-            grad_s[:, low + kw : low + kw + HD] = mul(
+            grad_s[:length, low : low + HD] = mul(d_scores, qg, FIRST).astype(bf16)
+            grad_s[:length, low + kw : low + kw + HD] = mul(
                 probs.astype(bf16), ag, FIRST
             ).astype(bf16)
 
@@ -373,41 +375,104 @@
         if t == 0:
             filled(w_s.at[b], w_sem.at[i])
 
-    def scatter(t):
-        weights_wait(t, 0, diag)
+    def lanes_of(h):
+        low, count = groups[h]
+        return slice(low * cw, (low + count) * cw)
+
+    def scatter_first():
+        rows = grad_s[:length]
+        weights_wait(0, 0, diag)
         for h in range(len(groups)):
-            for c, term in pieces(partial(diag, *groups[h], grad_s[...]), *groups[h]):
-                send_s[t, 0, c] = term.astype(bf16)
-            rs_copy(t, 0, h, partner).start()
-        if t == 1:
-            cross_start(1, lane_sum(grad_s[...].astype(f32) * proj_s[...]))
-        weights_wait(t, 1, across)
+            for c, term in pieces(partial(diag, *groups[h], rows), *groups[h]):
+                send_s[0, 0, c] = term.astype(bf16)
+            rs_copy(0, 0, h, partner).start()
+        weights_wait(0, 1, across)
         for h in range(len(groups)):
-            terms = pieces(partial(across, *groups[h], grad_s[...]), *groups[h])
-            rs_copy(t, 0, h, partner).wait_recv()
+            terms = pieces(partial(across, *groups[h], rows), *groups[h])
+            rs_copy(0, 0, h, partner).wait_recv()
             for c, term in terms:
-                send_s[t, 1, c] = (term + recv_s[t, 0, c].astype(f32)).astype(bf16)
-            if t == 0:
-                rs_copy(t, 1, h, across).start()
-        if t == 1:
+                send_s[0, 1, c] = (term + recv_s[0, 0, c].astype(f32)).astype(bf16)
+            for c, _ in terms:
+                rs_copy(0, 1, c, across).start()
+        weights_wait(0, 2, partner)
+        for c, term in pieces(partial(partner, 0, chunks, rows), 0, chunks):
+            send_s[0, 2, c] = term.astype(bf16)
+        for h in range(len(groups)):
+            rs_copy(0, 2, h, partner).start()
+        weights_wait(0, 3, me)
+        term_s[...] = partial(me, 0, chunks, rows)
+
+    def scatter_last(handed):
+        pick_of = chosen(1).astype(bf16)
+        rstd = rstd_s[:, 0:1]
+
+        def pass_on(i, h, term):
+            for c, piece in pieces(term, *groups[h]):
+                send_s[1, i, c] = piece.astype(bf16)
+            rs_copy(1, i, h, partner).start()
+
+        def pass_rows(i, h, rows):
+            sel_s[i, h] = rows.astype(bf16)
+            sel_copy(i, h).start()
+
+        grad_s[length:] = mul(pick_of, grad_s[:length], FIRST).astype(bf16)
+        every = grad_s[...]
+        cross_start(1, lane_sum(grad_s[:length].astype(f32) * proj_s[...]))
+        def far_part(h):
+            term = partial(across, *groups[h], every)
+            sel_copy(0, h).wait_recv()
+            rows = term[length:] + sel_r[0, h].astype(f32)
+            gain_far = gain_r[:, lanes_of(h)].astype(f32)
+            rows_s[0, h] = (rstd * (gain_far * rows)).astype(bf16)
 
             @pl.when(section == 0)
             def _():
-                sums = jnp.concatenate([send_s[1, 1, c] for c in range(chunks)], axis=1)
-                sums = as_column(rstd_lanes(1)) * (gain_r[...].astype(f32) * sums.astype(f32))
-                rows_s[0] = mul(chosen(1), sums.astype(bf16), FIRST).astype(bf16)
                 for o in range(n_section - 1, -1, -1):
-                    far_rows(o).start()
-
-            for h in range(len(groups)):
-                rs_copy(t, 1, h, across).start()
-        weights_wait(t, 2, partner)
-        for c, term in pieces(partial(partner, 0, chunks, grad_s[...]), 0, chunks):
-            send_s[t, 2, c] = term.astype(bf16)
+                    far_rows(h, o).start()
+
+            rs_copy(1, 0, h, partner).wait_recv()
+            for c, piece in pieces(term[:length], *groups[h]):
+                send_s[1, 1, c] = (piece + recv_s[1, 0, c].astype(f32)).astype(bf16)
+
+        def own_part(h, rows):
+            at = lanes_of(h)
+            sel_copy(1, h).wait_recv()
+            rows = rstd * (gains[:, at] * (rows + sel_r[1, h].astype(f32)))
+            rows_s[1, h] = (bases_s[:, at] + rows).astype(bf16)
+
+            @pl.when(section == 0)
+            def _():
+                for o in range(1, n_section):
+                    own_rows_copy(h, o).start()
+
         for h in range(len(groups)):
-            rs_copy(t, 2, h, partner).start()
-        weights_wait(t, 3, me)
-        term_s[...] = partial(me, 0, chunks, grad_s[...])
+            term = partial(diag, *groups[h], every)
+            pass_rows(0, h, term[length:])
+            pass_on(0, h, term[:length])
+        for h in range(len(groups)):
+            far_part(h)
+        for c in range(chunks):
+            rs_copy(1, 1, c, across).start()
+        term = partial(partner, *groups[0], every)
+        pass_rows(1, 0, term[length:])
+        pass_on(2, 0, term[:length])
+        cross = cross_wait(1)
+        inverse = rstd_lanes(1)
+        terms = [partial(partner, *groups[h], every) for h in range(1, len(groups))]
+        factor = as_column(inverse * inverse * inverse * (cross / depth))
+        for c in range(chunks):
+            at = slice(c * cw, (c + 1) * cw)
+            below = g_s[1, me, c].astype(f32) - handed * upper_s[me, :, at].astype(f32)
+            base_s[:, at] = below - x_s[1, :, at].astype(f32) * factor
+        for h, term in enumerate(terms, 1):
+            pass_rows(1, h, term[length:])
+            pass_on(2, h, term[:length])
+        for h in range(len(groups)):
+            term = partial(me, *groups[h], every)
+            if h == 0:
+                bases_s[...] = mul(pick_of, base_s[...].astype(bf16), FIRST)
+            term_s[:, lanes_of(h)] = term[:length]
+            own_part(h, term[length:])
 
     def rstd_lanes(t):
         squares = square_s[t] + square_r[0, t] + square_r[1, t] + square_r[2, t]
@@ -419,15 +484,17 @@
 
     def pick_first():
         rows = jnp.concatenate([out_s[0, c] for c in range(chunks)], axis=1)
-        picks[seq, 0] = mul(chosen(0), rows, FIRST).astype(bf16)
+        rows = mul(chosen(0).astype(bf16), rows, FIRST).astype(bf16)
+        for h in range(len(groups)):
+            picks[seq, 0, h] = rows[:, lanes_of(h)]
         for o in range(1, n_section):
             pick_spread(o).start()
 
-    def picks_join(own):
-        far_rows(0).wait_recv()
-        picks[seq, 1] = (own.astype(f32) + rows_r[0].astype(f32)).astype(bf16)
+    def picks_join(h, own):
+        far_rows(h, 0).wait_recv()
+        picks[seq, 1, h] = (own.astype(f32) + rows_r[0, h].astype(f32)).astype(bf16)
         for o in range(1, n_dp):
-            pick_copy(1, o).start()
+            pick_copy(picks.at[seq, 1, h], o).start()
 
     loads["wo0"].wait()
     d_attn = wo_part(0, me, 0, chunks)
@@ -449,7 +516,7 @@
     d_attn += wo_part(0, diag, chunks - 1)
     attn_s[...] = d_attn.astype(bf16)
     attention(0)
-    scatter(0)
+    scatter_first()
     loads["feat"].wait()
     for j in range(n_dp):
         for t in range(TICKS):
@@ -461,27 +528,33 @@
         feat_copy(o).start()
 
     landed(square_r, R_SQUARE)
+    loads["pos"].wait()
+    rstd_s[...] = lax.dot_general(
+        chosen(1), jnp.broadcast_to(as_column(rstd_lanes(1)), (length, LANES)), FIRST,
+        precision=lax.Precision.HIGHEST, preferred_element_type=f32,
+    )
     rstd = as_column(rstd_lanes(0))
     total = jnp.zeros((length, LANES), f32)
-    for h, (low, count) in enumerate(groups):
-        if h == 0:
-            landed(recv_s.at[0, 2], rs_recv.at[0, 2 * len(groups)])
-        rs_copy(0, 1, h, across).wait_recv()
-        for c in range(low, low + count):
-            at = slice(c * cw, (c + 1) * cw)
-            weighted = gains[:, at] * d_normed(0, c)
-            total += lane_sum(x_s[0, :, at].astype(f32) * weighted)
-            passed = g_s[0, me, c].astype(f32) + rstd * weighted
-            out_s[0, c] = passed.astype(bf16)
-            term_s[:, at] = passed
+    landed(recv_s.at[0, 2], rs_recv.at[0, len(groups) + chunks])
+    for c in range(chunks):
+        rs_copy(0, 1, c, across).wait_recv()
+        at = slice(c * cw, (c + 1) * cw)
+        weighted = gains[:, at] * d_normed(0, c)
+        passed = g_s[0, me, c].astype(f32) + rstd * weighted
+        out_s[0, c] = passed.astype(bf16)
 
         @pl.when(section > 0)
         def _():
-            for c in range(low, low + count):
-                if c in direct:
-                    held_far(c).start()
-            for c in range(low, low + count):
+            if c in early:
                 held_copy(c).start()
+            else:
+                held_far(c).start()
+            if c == late[-1]:
+                for b in late:
+                    held_copy(b).start()
+
+        term_s[:, at] = passed
+        total += lane_sum(x_s[0, :, at].astype(f32) * weighted)
 
     cross_start(0, total)
 
@@ -516,11 +589,13 @@
         for c in early:
             received(c)
 
-    loads["pos"].wait()
-
     pair = stacked(me, early[0], len(early))
     landed(g_s.at[1, partner, first_span], near_recv.at[1])
     pair += stacked(partner, early[0], len(early))
+
+    for c in late:
+        forward(1, c)
+    pair += stacked(across, late[0], len(late))
 
     @pl.when(section == 0)
     def _():
@@ -531,9 +606,6 @@
             out_s[0, c] = (term_s[:, at] - x_s[0, :, at].astype(f32) * factor).astype(bf16)
         pick_first()
 
-    for c in late:
-        forward(1, c)
-    pair += stacked(across, late[0], len(late))
     landed(g_s.at[1, diag, later_span], diag_recv.at[chunks + 1])
     pair += stacked(diag, late[0], len(late))
     for c in late:
@@ -564,40 +636,28 @@
         pick_spread(0).wait_recv()
 
     for o in range(1, n_dp):
-        pick_copy(0, o).start()
+        pick_copy(picks.at[seq, 0], o).start()
     attention(1)
     gain_copy.wait_recv()
-    scatter(1)
-    rstd = rstd_lanes(1)
-    factor = as_column(rstd * rstd * rstd * (cross_wait(1) / depth))
-    rstd = as_column(rstd)
-    landed(recv_s.at[1, 2], rs_recv.at[1, 2 * len(groups)])
+    scatter_last(handed)
+
+    @pl.when(section == 0)
+    def _():
+        for h in range(len(groups)):
+            picks_join(h, rows_s[1, h])
+
+    @pl.when(section > 0)
+    def _():
+        for h in range(len(groups)):
+            own_rows_copy(h, 0).wait_recv()
+            picks_join(h, rows_r[1, h])
+
+    rstd = as_column(rstd_lanes(1))
+    landed(recv_s.at[1, 2], rs_recv.at[1, len(groups) + chunks])
     for c in range(chunks):
+        rs_copy(1, 1, c, across).wait_recv()
         at = slice(c * cw, (c + 1) * cw)
-        below = g_s[1, me, c].astype(f32) - handed * upper_s[me, :, at].astype(f32)
-        local = term_s[:, at] + recv_s[1, 2, c].astype(f32)
-        change = rstd * (gains[:, at] * local) - x_s[1, :, at].astype(f32) * factor
-        term_s[:, at] = below + change
-
-    @pl.when(section == 0)
-    def _():
-        rows_s[1] = mul(chosen(1), term_s[...].astype(bf16), FIRST).astype(bf16)
-        for o in range(1, n_section):
-            own_rows_copy(o).start()
-        picks_join(rows_s[1])
-
-    for h, (low, count) in enumerate(groups):
-        rs_copy(1, 1, h, across).wait_recv()
-        for c in range(low, low + count):
-            at = slice(c * cw, (c + 1) * cw)
-            out_s[1, c] = (
-                term_s[:, at] + rstd * (gains[:, at] * recv_s[1, 1, c].astype(f32))
-            ).astype(bf16)
-
-    @pl.when(section > 0)
-    def _():
-        own_rows_copy(0).wait_recv()
-        picks_join(rows_r[1])
+        out_s[1, c] = (base_s[:, at] + rstd * (gains[:, at] * d_normed(1, c))).astype(bf16)
 
     for c in range(chunks):
         pending[0, 0, :, c * cw : (c + 1) * cw] = out_s[1, c]
@@ -610,6 +670,7 @@
     drain(cross_r, S_CROSS)
     drain(square_r, S_SQUARE)
     drain(gain_s, S_GAIN)
+    drain(sel_s, S_CHOSEN)
 
     @pl.when(section == last)
     def _():
@@ -645,10 +706,13 @@
     handed.start()
     band = out.shape[0] // bands
     lhs = feat[...].T
+    rhs = jnp.concatenate(
+        [picked[:, h].reshape(-1, picked.shape[3]) for h in range(picked.shape[1])], axis=1
+    )
     copies = []
     for i in range(bands):
         rows = pl.ds(i * band, band)
-        out_s[rows, :] = mul(lhs[i * band : (i + 1) * band], picked[...], PLAIN).astype(out_s.dtype)
+        out_s[rows, :] = mul(lhs[i * band : (i + 1) * band], rhs, PLAIN).astype(out_s.dtype)
         copies.append(pltpu.make_async_copy(out_s.at[rows], out.at[rows], out_sem.at[i]))
         copies[-1].start()
     for copy in copies:
@@ -668,13 +732,14 @@
     group = width // kw
     images = features.shape[2]
     own_rows = features.shape[3] // n_dp
+    halves = len(groups)
     f32, bf16 = jnp.float32, jnp.bfloat16
     vmem, dma = pltpu.VMEM, pltpu.SemaphoreType.DMA
     feat_all, picks, pending = pl.pallas_call(
         functools.partial(kernel, n_section, n_dp, n_mp, chunks, direct, groups),
         out_shape=(
             jax.ShapeDtypeStruct((n_dp, TICKS * images, own_rows), bf16),
-            jax.ShapeDtypeStruct((n_dp, TICKS, images, width), bf16),
+            jax.ShapeDtypeStruct((n_dp, TICKS, halves, images, width // halves), bf16),
             jax.ShapeDtypeStruct((1, 1, length, width), bf16),
         ),
         in_specs=[pl.BlockSpec(memory_space=pltpu.HBM)] * 13,
@@ -693,7 +758,7 @@
             vmem((TICKS, images), jnp.int32),
             vmem((TICKS, kv_local, group * length, length), f32),
             vmem((length, width), bf16),
-            vmem((length, width + 2 * kw), bf16),
+            vmem((length + images, width + 2 * kw), bf16),
             vmem((TICKS, chunks, length, width // chunks), bf16),
             vmem((TICKS, 3, chunks, length, width // chunks), bf16),
             vmem((TICKS, 3, chunks, length, width // chunks), bf16),
@@ -708,12 +773,17 @@
             vmem((8, LANES), f32),
             vmem((8, LANES), f32),
             vmem((1, width), bf16),
-            vmem((2, images, width), bf16),
-            vmem((2, images, width), bf16),
-            dma((9,)), dma((n_mp,)), dma((n_mp,)), dma((17,)),
+            vmem((2, halves, images, width // halves), bf16),
+            vmem((2, halves, images, width // halves), bf16),
+            vmem((length, width), f32),
+            vmem((2, halves, images, width // halves), bf16),
+            vmem((2, halves, images, width // halves), bf16),
+            vmem((images, LANES), f32),
+            vmem((images, width), f32),
+            dma((9,)), dma((n_mp,)), dma((n_mp,)), dma((18,)),
             dma((TICKS, chunks)), dma((3,)), dma((chunks + 2,)),
-            dma((3,)), dma((4,)), dma((TICKS, 2 * len(groups) + 1)), dma((TICKS,)),
-            dma((8,)), dma((chunks,)),
+            dma((3,)), dma((4,)), dma((TICKS, len(groups) + chunks + 1)), dma((TICKS,)),
+            dma((6,)), dma((chunks,)), dma((2, halves)), dma((halves,)), dma((halves,)),
         ],
         compiler_params=pltpu.CompilerParams(
             collective_id=0, has_side_effects=True, vmem_limit_bytes=48 * 2**20
@@ -739,7 +809,7 @@
             vmem((own_rows, width), bf16), dma((bands,)), dma(()),
         ],
         compiler_params=pltpu.CompilerParams(vmem_limit_bytes=8 * 2**20),
-    )(feat_all.reshape(-1, own_rows), picks.reshape(-1, width), pending)
+    )(feat_all.reshape(-1, own_rows), picks.reshape((-1,) + picks.shape[2:]), pending)
 
 
 def solution(mesh):

time: 41.4 us -> 40.6 us (0.981)
  Pallas kernels: 40.6 us -> 39.7 us
    pallas_call x1, Pallas kernels: 39 us -> 38.1 us  [shards(): pl.pallas_call(functools.partial(kernel, n_section, n_dp, n_mp, chunks, d...]
where the time goes in v4:
time: 40.6 us; the launch traced here: 40.5 us
  Pallas kernels  39.7 us (98%)
  between operations  0.8 us (2%)
    pallas_call x1, Pallas kernels, shards(): pl.pallas_call(functools.partial(kernel, n_section, n_dp, n_mp, chunks, d...  38.1 us
    pallas_call x1, Pallas kernels, shards(): pl.pallas_call(functools.partial(project_kernel, bands), out_shape=(jax.S...  1.61 us

profile of v4, /device:TPU:0, one launch (start us, length us, event | category | flops | bytes accessed | tf_op | source)
XLA Modules:
  0.0 40.5 jit_solution(18051709318422136946)
XLA Ops:
  0.6 38.1 %shard_map.140 = (bf16[4,32,960]{2,1,0:T(8,128)(2,1)S(1)}, bf16[4,2,2,16,512]{4,3,2,1,0:T(8,128)(2,1)S(1)}, bf16[1,1,64,1024]{3,2,1,0:T(8,128)(2,1)S(1)}) custom-call(bf16[1,4096,1024]{2,1,0:T(8,128)(2,1)} %wq.1, bf16[1,4096,256]{2,1,0:T(8,128)(2,1)} %wk.1, bf16[1,4096,256]{2,1,0:T(8,128)(2,1)} %wv.1, bf16[1,1024,4096]{2,1,0:T(8,128)(2,1)} %wo.1, ...), custom_call_target="tpu_custom_call" | custom-call | tf_op jit(solution)/shard_map/pallas_call | solution.py:738
  38.7 1.6 %shard_map.141 = (bf16[960,1024]{1,0:T(8,128)(2,1)}, bf16[1,1,64,1024]{3,2,1,0:T(8,128)(2,1)}) custom-call(bf16[128,960]{1,0:T(8,128)(2,1)S(1)} %bitcast.2, bf16[8,2,16,512]{3,2,1,0:T(8,128)(2,1)S(1)} %bitcast.3, bf16[1,1,64,1024]{3,2,1,0:T(8,128)(2,1)S(1)} %get-tuple-element.7.pending), custom_call_target="tpu_custom_call" | custom-call | tf_op jit(solution)/shard_map/pallas_call | solution.py:800

commit v5 on v4

--- a/solution.py
+++ b/solution.py
@@ -30,7 +30,7 @@
     wq, wk, wv, wo, gain, x, q, k, v, g_in, fresh, feat, pos,
     feat_all, picks, pending,
     w_s, wo_s, gain_s, x_s, q_s, k_s, v_s, g_s, feat_s, cut_s, pos_s,
-    probs_s, attn_s, grad_s, out_s, send_s, recv_s, term_s,
+    probs_s, mixed_s, turned_s, attn_s, grad_s, out_s, send_s, recv_s, term_s,
     scaled_s, upper_s, proj_s, cross_s, cross_r, square_s, square_r, factor_s, factor_r,
     gain_r, rows_s, rows_r, base_s, sel_s, sel_r, rstd_s, bases_s,
     load_sem, wo_sem, w_sem, out_sem, across_recv, near_recv, diag_recv,
@@ -239,7 +239,13 @@
             scores = mul(stack(q_s[t], g), kg, LAST) * scale
             scores = jnp.where(causal, scores, -1e30)
             expo = jnp.exp(scores - jnp.max(scores, -1, keepdims=True))
-            probs_s[t, g] = expo / jnp.sum(expo, -1, keepdims=True)
+            probs = expo / jnp.sum(expo, -1, keepdims=True)
+            probs_s[t, g] = probs
+            vg = v_s[t, :, g * HD : (g + 1) * HD].astype(f32)
+            mixed_s[t, g] = lax.dot_general(
+                probs, vg, PLAIN, precision=lax.Precision.HIGHEST, preferred_element_type=f32
+            )
+            turned_s[t, g] = probs.astype(bf16).T
 
     for t in range(TICKS):
         softmax(t)
@@ -352,7 +358,7 @@
             ag = stack(attn_s[...], g)
             probs = probs_s[t, g]
             d_probs = mul(ag, vg, LAST)
-            inner = jnp.sum(probs * d_probs, -1, keepdims=True)
+            inner = jnp.sum(ag.astype(f32) * mixed_s[t, g], -1, keepdims=True)
             d_scores = (probs * (d_probs - inner) * scale).astype(bf16)
             d_query = mul(d_scores, kg, PLAIN).astype(bf16)
             for j in range(group):
@@ -362,7 +368,7 @@
             low = width + g * HD
             grad_s[:length, low : low + HD] = mul(d_scores, qg, FIRST).astype(bf16)
             grad_s[:length, low + kw : low + kw + HD] = mul(
-                probs.astype(bf16), ag, FIRST
+                turned_s[t, g], ag, PLAIN
             ).astype(bf16)
 
     def partial(b, low, count, rows):
@@ -757,6 +763,8 @@
             vmem((n_dp, TICKS * images, own_rows), bf16),
             vmem((TICKS, images), jnp.int32),
             vmem((TICKS, kv_local, group * length, length), f32),
+            vmem((TICKS, kv_local, group * length, HD), f32),
+            vmem((TICKS, kv_local, length, group * length), bf16),
             vmem((length, width), bf16),
             vmem((length + images, width + 2 * kw), bf16),
             vmem((TICKS, chunks, length, width // chunks), bf16),

time: 40.6 us -> 40.3 us (level)
  no operation moved by 1% of the time
where the time goes in v5:
time: 40.3 us; the launch traced here: 40.2 us
  Pallas kernels  39.3 us (98%)
  between operations  0.8 us (2%)
    pallas_call x1, Pallas kernels, shards(): pl.pallas_call(functools.partial(kernel, n_section, n_dp, n_mp, chunks, d...  37.7 us
    pallas_call x1, Pallas kernels, shards(): pl.pallas_call(functools.partial(project_kernel, bands), out_shape=(jax.S...  1.6 us

profile of v5, /device:TPU:0, one launch (start us, length us, event | category | flops | bytes accessed | tf_op | source)
XLA Modules:
  0.0 40.2 jit_solution(17830456971970424359)
XLA Ops:
  0.6 37.7 %shard_map.140 = (bf16[4,32,960]{2,1,0:T(8,128)(2,1)S(1)}, bf16[4,2,2,16,512]{4,3,2,1,0:T(8,128)(2,1)S(1)}, bf16[1,1,64,1024]{3,2,1,0:T(8,128)(2,1)S(1)}) custom-call(bf16[1,4096,1024]{2,1,0:T(8,128)(2,1)} %wq.1, bf16[1,4096,256]{2,1,0:T(8,128)(2,1)} %wk.1, bf16[1,4096,256]{2,1,0:T(8,128)(2,1)} %wv.1, bf16[1,1024,4096]{2,1,0:T(8,128)(2,1)} %wo.1, ...), custom_call_target="tpu_custom_call" | custom-call | tf_op jit(solution)/shard_map/pallas_call | solution.py:744
  38.4 1.6 %shard_map.141 = (bf16[960,1024]{1,0:T(8,128)(2,1)}, bf16[1,1,64,1024]{3,2,1,0:T(8,128)(2,1)}) custom-call(bf16[128,960]{1,0:T(8,128)(2,1)S(1)} %bitcast.2, bf16[8,2,16,512]{3,2,1,0:T(8,128)(2,1)S(1)} %bitcast.3, bf16[1,1,64,1024]{3,2,1,0:T(8,128)(2,1)S(1)} %get-tuple-element.7.pending), custom_call_target="tpu_custom_call" | custom-call | tf_op jit(solution)/shard_map/pallas_call | solution.py:808

commit v6 on v5

--- a/solution.py
+++ b/solution.py
@@ -68,6 +68,24 @@
             device_id=where, device_id_type=MESH,
         )
 
+    barrier = pltpu.get_barrier_semaphore()
+    for b in (partner, across, diag):
+        pl.semaphore_signal(barrier, inc=1, device_id={"mp": b}, device_id_type=MESH)
+    for o in range(1, n_dp):
+        pl.semaphore_signal(
+            barrier, inc=1, device_id={"dp": (seq + o) % n_dp}, device_id_type=MESH
+        )
+    greets = n_mp - 1 + n_dp - 1 + n_section - 1
+    for o in range(1, n_section):
+        other = (section + o) % n_section
+        pl.semaphore_signal(
+            barrier, inc=1, device_id={"section": other}, device_id_type=MESH
+        )
+        pl.semaphore_signal(
+            barrier, inc=1, device_id={"section": other, "mp": across}, device_id_type=MESH
+        )
+        greets += 1
+
     loads = {}
 
     def load(name, src, dst, sem):
@@ -100,23 +118,6 @@
     for i, b in enumerate(order):
         columns = pl.ds(pl.multiple_of(b * width, width), width)
         load(f"wo{i}", wo.at[0, :, columns], wo_s.at[b], wo_sem.at[i])
-    barrier = pltpu.get_barrier_semaphore()
-    for b in (partner, across, diag):
-        pl.semaphore_signal(barrier, inc=1, device_id={"mp": b}, device_id_type=MESH)
-    for o in range(1, n_dp):
-        pl.semaphore_signal(
-            barrier, inc=1, device_id={"dp": (seq + o) % n_dp}, device_id_type=MESH
-        )
-    greets = n_mp - 1 + n_dp - 1 + n_section - 1
-    for o in range(1, n_section):
-        other = (section + o) % n_section
-        pl.semaphore_signal(
-            barrier, inc=1, device_id={"section": other}, device_id_type=MESH
-        )
-        pl.semaphore_signal(
-            barrier, inc=1, device_id={"section": other, "mp": across}, device_id_type=MESH
-        )
-        greets += 1
     pl.semaphore_wait(barrier, greets)
 
     def block_copy(ref, ssem, rsem, where):
@@ -165,6 +166,7 @@
     filled(g_s.at[0, me], load_sem.at[0])
     for c in range(chunks):
         to_across(0, c).start()
+    for c in range(chunks):
         to_partner(0, c).start()
     for i, b in enumerate((diag, across, partner, me)):
         rows = pl.ds(pl.multiple_of(b * width, width), width)
@@ -509,8 +511,9 @@
     d_attn += wo_part(0, partner, 0, chunks)
     for c in range(chunks):
         forward(0, c)
+        if c == 1:
+            inputs_start()
         if c == 0:
-            inputs_start()
             loads["wo2"].wait()
         d_attn += wo_part(0, across, c)
         if c > 0:

time: 40.3 us -> 40.3 us (level)
  no operation moved by 1% of the time
where the time goes in v6:
time: 40.3 us; the launch traced here: 40.1 us
  Pallas kernels  39.3 us (98%)
  between operations  0.8 us (2%)
    pallas_call x1, Pallas kernels, shards(): pl.pallas_call(functools.partial(kernel, n_section, n_dp, n_mp, chunks, d...  37.7 us
    pallas_call x1, Pallas kernels, shards(): pl.pallas_call(functools.partial(project_kernel, bands), out_shape=(jax.S...  1.6 us

profile of v6, /device:TPU:0, one launch (start us, length us, event | category | flops | bytes accessed | tf_op | source)
XLA Modules:
  0.0 40.1 jit_solution(15656208092371963766)
XLA Ops:
  0.6 37.7 %shard_map.140 = (bf16[4,32,960]{2,1,0:T(8,128)(2,1)S(1)}, bf16[4,2,2,16,512]{4,3,2,1,0:T(8,128)(2,1)S(1)}, bf16[1,1,64,1024]{3,2,1,0:T(8,128)(2,1)S(1)}) custom-call(bf16[1,4096,1024]{2,1,0:T(8,128)(2,1)} %wq.1, bf16[1,4096,256]{2,1,0:T(8,128)(2,1)} %wk.1, bf16[1,4096,256]{2,1,0:T(8,128)(2,1)} %wv.1, bf16[1,1024,4096]{2,1,0:T(8,128)(2,1)} %wo.1, ...), custom_call_target="tpu_custom_call" | custom-call | tf_op jit(solution)/shard_map/pallas_call | solution.py:747
  38.3 1.6 %shard_map.141 = (bf16[960,1024]{1,0:T(8,128)(2,1)}, bf16[1,1,64,1024]{3,2,1,0:T(8,128)(2,1)}) custom-call(bf16[128,960]{1,0:T(8,128)(2,1)S(1)} %bitcast.2, bf16[8,2,16,512]{3,2,1,0:T(8,128)(2,1)S(1)} %bitcast.3, bf16[1,1,64,1024]{3,2,1,0:T(8,128)(2,1)S(1)} %get-tuple-element.7.pending), custom_call_target="tpu_custom_call" | custom-call | tf_op jit(solution)/shard_map/pallas_call | solution.py:811

commit v7 on v6

--- a/solution.py
+++ b/solution.py
@@ -28,11 +28,11 @@
 def kernel(
     n_section, n_dp, n_mp, chunks, direct, groups,
     wq, wk, wv, wo, gain, x, q, k, v, g_in, fresh, feat, pos,
-    feat_all, picks, pending,
+    feat_turned, picks, pending,
     w_s, wo_s, gain_s, x_s, q_s, k_s, v_s, g_s, feat_s, cut_s, pos_s,
     probs_s, mixed_s, turned_s, attn_s, grad_s, out_s, send_s, recv_s, term_s,
     scaled_s, upper_s, proj_s, cross_s, cross_r, square_s, square_r, factor_s, factor_r,
-    gain_r, rows_s, rows_r, base_s, sel_s, sel_r, rstd_s, bases_s,
+    gain_r, feat_all, rows_s, rows_r, base_s, sel_s, sel_r, rstd_s, bases_s,
     load_sem, wo_sem, w_sem, out_sem, across_recv, near_recv, diag_recv,
     xg_recv, up_recv, rs_recv, cr_recv, row_recv, held_recv, sel_recv, far_recv, own_recv,
 ):
@@ -661,6 +661,8 @@
             own_rows_copy(h, 0).wait_recv()
             picks_join(h, rows_r[1, h])
 
+    landed(feat_all.at[pl.ds(0, n_dp - 1)], R_FEAT)
+    feat_turned[...] = feat_all[...].reshape(-1, own_rows).T
     rstd = as_column(rstd_lanes(1))
     landed(recv_s.at[1, 2], rs_recv.at[1, len(groups) + chunks])
     for c in range(chunks):
@@ -705,7 +707,6 @@
 
     others = pl.ds(0, n_dp - 1)
     drain(feat_all.at[others], S_FEAT)
-    landed(feat_all.at[others], R_FEAT)
     drain(picks.at[others], S_PICK)
     landed(picks.at[others], R_PICK)
 
@@ -714,14 +715,13 @@
     handed = pltpu.make_async_copy(pending, pending_out, pending_sem)
     handed.start()
     band = out.shape[0] // bands
-    lhs = feat[...].T
     rhs = jnp.concatenate(
         [picked[:, h].reshape(-1, picked.shape[3]) for h in range(picked.shape[1])], axis=1
     )
     copies = []
     for i in range(bands):
         rows = pl.ds(i * band, band)
-        out_s[rows, :] = mul(lhs[i * band : (i + 1) * band], rhs, PLAIN).astype(out_s.dtype)
+        out_s[rows, :] = mul(feat[rows, :], rhs, PLAIN).astype(out_s.dtype)
         copies.append(pltpu.make_async_copy(out_s.at[rows], out.at[rows], out_sem.at[i]))
         copies[-1].start()
     for copy in copies:
@@ -747,7 +747,7 @@
     feat_all, picks, pending = pl.pallas_call(
         functools.partial(kernel, n_section, n_dp, n_mp, chunks, direct, groups),
         out_shape=(
-            jax.ShapeDtypeStruct((n_dp, TICKS * images, own_rows), bf16),
+            jax.ShapeDtypeStruct((own_rows, n_dp * TICKS * images), bf16),
             jax.ShapeDtypeStruct((n_dp, TICKS, halves, images, width // halves), bf16),
             jax.ShapeDtypeStruct((1, 1, length, width), bf16),
         ),
@@ -784,6 +784,7 @@
             vmem((8, LANES), f32),
             vmem((8, LANES), f32),
             vmem((1, width), bf16),
+            vmem((n_dp, TICKS * images, own_rows), bf16),
             vmem((2, halves, images, width // halves), bf16),
             vmem((2, halves, images, width // halves), bf16),
             vmem((length, width), f32),
@@ -820,7 +821,7 @@
             vmem((own_rows, width), bf16), dma((bands,)), dma(()),
         ],
         compiler_params=pltpu.CompilerParams(vmem_limit_bytes=8 * 2**20),
-    )(feat_all.reshape(-1, own_rows), picks.reshape((-1,) + picks.shape[2:]), pending)
+    )(feat_all, picks.reshape((-1,) + picks.shape[2:]), pending)
 
 
 def solution(mesh):

time: 40.3 us -> 40.2 us (level)
  no operation moved by 1% of the time
where the time goes in v7:
time: 40.2 us; the launch traced here: 40.1 us
  Pallas kernels  39.3 us (98%)
  between operations  0.8 us (2%)
    pallas_call x1, Pallas kernels, shards(): pl.pallas_call(functools.partial(kernel, n_section, n_dp, n_mp, chunks, d...  37.7 us
    pallas_call x1, Pallas kernels, shards(): pl.pallas_call(functools.partial(project_kernel, bands), out_shape=(jax.S...  1.57 us

profile of v7, /device:TPU:0, one launch (start us, length us, event | category | flops | bytes accessed | tf_op | source)
XLA Modules:
  0.0 40.1 jit_solution(695105199511718412)
XLA Ops:
  0.6 37.7 %shard_map.140 = (bf16[960,128]{1,0:T(8,128)(2,1)S(1)}, bf16[4,2,2,16,512]{4,3,2,1,0:T(8,128)(2,1)S(1)}, bf16[1,1,64,1024]{3,2,1,0:T(8,128)(2,1)S(1)}) custom-call(bf16[1,4096,1024]{2,1,0:T(8,128)(2,1)} %wq.1, bf16[1,4096,256]{2,1,0:T(8,128)(2,1)} %wk.1, bf16[1,4096,256]{2,1,0:T(8,128)(2,1)} %wv.1, bf16[1,1024,4096]{2,1,0:T(8,128)(2,1)} %wo.1, ...), custom_call_target="tpu_custom_call" | custom-call | tf_op jit(solution)/shard_map/pallas_call | solution.py:747
  38.3 1.6 %shard_map.141 = (bf16[960,1024]{1,0:T(8,128)(2,1)}, bf16[1,1,64,1024]{3,2,1,0:T(8,128)(2,1)}) custom-call(bf16[960,128]{1,0:T(8,128)(2,1)S(1)} %get-tuple-element.5.feat, bf16[8,2,16,512]{3,2,1,0:T(8,128)(2,1)S(1)} %bitcast.1, bf16[1,1,64,1024]{3,2,1,0:T(8,128)(2,1)S(1)} %get-tuple-element.7.pending), custom_call_target="tpu_custom_call" | custom-call | tf_op jit(solution)/shard_map/pallas_call | solution.py:812
